TPU v7x, 128 devices: a whole 4x4x4 slice. The times are simulated.
128 devices in a mesh: req: 16 (over x, z), head: 8 (over y, core).
Axes of the slice: x: 4, y: 4, z: 4, core: 2. Of those that a mesh axis runs over, the one named last changes fastest.
Arguments:
- hidden_in: bfloat16 [16384, 1536], P(('req', 'head')), may hold values from -3 to 3
- attn_gain: float32 [1536], replicated, may hold values from 0.1 to 1.9
- w_query: bfloat16 [1536, 1536], P(None, 'head'), may hold values from -0.15625 to 0.15625
- keyvalue_weight: bfloat16 [1536, 8, 128], P(None, 'head'), may hold values from -0.3125 to 0.3125
- w_out: bfloat16 [1536, 1536], P('head'), may hold values from -0.375 to 0.375
- cache_kv: bfloat16 [64, 2048, 8, 128], P('req', None, 'head'), may hold values from -400 to 400
- ctx_len: int32 [64], replicated, may hold values from 2 to 2048, as said below
- span_len: int32 [16, 4], replicated, may hold values from 1 to 512, 1024 in all within a row
- ffn_gain: float32 [1536], replicated, may hold values from 0.1 to 1.9
- routes: int32 [16384, 8], P(('req', 'head')), may hold values from 0 to 31, all different within a row; in each aligned block of 128 rows (0 to 127, 128 to 255, ...) at most 48 rows name the same one
- gate_weights: bfloat16 [16384, 8], P(('req', 'head')), may hold values from 0.049804688 to 0.29882812
- w_gate_up: bfloat16 [32, 1536, 1024], P('req'), may hold values from -0.15625 to 0.15625
- w_down: bfloat16 [32, 512, 1536], P('req'), may hold values from -0.25 to 0.25
- req_prompt: int32 [288], P('req'), may hold values from 0 to 63
- cache_slot: int32 [288], P('req'), may hold values from 0 to 17, as said below
Outputs:
- layer_out: bfloat16 [16384, 1536], P(('req', 'head'))
- keyvalue_slot_cache: bfloat16 [288, 512, 8, 128], P('req', None, 'head')
Inputs may be any that keep to these rules, and one draw needn't show every extreme that they name: `span_len`: each row sums to 1024 and its largest entry is exactly 512. `ctx_len`: some prompt has exactly 2048 cached positions. `cache_slot`: within each block of 18 consecutive requests the entries are a permutation of 0 to 17. `routes`: each row names 8 different experts; within each aligned block of 128 rows no expert is named more than 48 times, and in some block some expert exactly 48 times.
All inputs are finite; a program needn't handle non-finite values.
Results may differ from a plain program's by a relative error of at most 0.0075.
The roundings to bfloat16 on the way count: a program that leaves them out, or rounds other values in their place, can miss the bound.
Values may be sent and summed in bfloat16 or wider, within the bound.
A program may use at most 128 MiB of HBM per device.

v0:
```python
import functools

import jax
import jax.numpy as jnp
from jax import lax
from jax.experimental import pallas as pl
from jax.experimental.pallas import tpu as pltpu
from jax.sharding import PartitionSpec as P

CAP = 48
EPSILON = 1e-05
ROPE_BASE = 10000.0
LOG2E = 1.4426950408889634
MESH = pl.DeviceIdType.MESH
F32 = jnp.float32
BF16 = jnp.bfloat16
VMEM_BYTES = 60 * 1024 * 1024


def vmem():
    return pl.BlockSpec(memory_space=pltpu.VMEM)


def smem():
    return pl.BlockSpec(memory_space=pltpu.SMEM)


def anyspace():
    return pl.BlockSpec(memory_space=pl.ANY)


def rms(values, gain):
    mean_sq = jnp.mean(values * values, axis=-1, keepdims=True)
    return values * lax.rsqrt(mean_sq + EPSILON) * gain


def head_neighbours():
    hd = lax.axis_index("head")
    y, c = hd // 2, hd % 2
    partner = y * 2 + (1 - c)
    up = ((y + 1) % 4) * 2 + c
    down = ((y + 3) % 4) * 2 + c
    return y, c, partner, up, down


def greet(neighbours):
    barrier = pltpu.get_barrier_semaphore()
    for axis, where in neighbours:
        pl.semaphore_signal(barrier, inc=1, device_id={axis: where}, device_id_type=MESH)
    return lambda: pl.semaphore_wait(barrier, len(neighbours))


def project_kernel(
    hidden_ref, gain_ref, wq_ref, wkv_ref, freq_ref, span_ref, ctx_ref,
    q_ref, kv_ref,
    tok, wq_wide, cos_tab, sin_tab, ssem, rsem,
):
    rows = hidden_ref.shape[0]
    half = rows // 2
    group = lax.axis_index("req")
    y, c, partner, up, down = head_neighbours()
    wait_all = greet([("head", partner), ("head", up), ("head", down)])
    tok[0] = rms(hidden_ref[...].astype(F32), gain_ref[...]).astype(BF16)
    wait_all()

    def copy(i, src, dst, to):
        return pltpu.make_async_remote_copy(
            src_ref=src, dst_ref=dst, send_sem=ssem.at[i], recv_sem=rsem.at[i],
            device_id={"head": to}, device_id_type=MESH,
        )

    low, high = pl.ds(0, half), pl.ds(half, half)
    copies = [
        copy(0, tok.at[0], tok.at[6], up),
        copy(1, tok.at[0], tok.at[2], down),
        copy(2, tok.at[0], tok.at[1], partner),
        copy(3, tok.at[6, low], tok.at[4, low], up),
        copy(4, tok.at[6], tok.at[7], partner),
        copy(5, tok.at[2, high], tok.at[4, high], down),
        copy(6, tok.at[2], tok.at[3], partner),
        copy(7, tok.at[4], tok.at[5], partner),
    ]
    for i in (0, 1, 2):
        copies[i].start()

    wq_wide[...] = jnp.zeros_like(wq_wide)
    for h in range(3):
        wq_wide[pl.ds(h * 128, 64), :] = wq_ref[pl.ds(h * 64, 64), :]

    lane = lax.broadcasted_iota(jnp.int32, (rows, 128), 1)

    @pl.loop(0, 8)
    def _(block):
        within = lax.broadcasted_iota(jnp.int32, (rows, 128), 0) + block * rows
        position = jnp.zeros((rows, 128), jnp.int32)
        begin = 0
        for j in range(4):
            shift = ctx_ref[group * 4 + j] - begin
            position = jnp.where(within >= begin, within + shift, position)
            begin = begin + span_ref[j, group]
        angles = position.astype(F32) * freq_ref[...]
        where_rows = pl.ds(pl.multiple_of(block * rows, rows), rows)
        cos_tab[where_rows, :] = jnp.where(lane < 64, jnp.cos(angles), 1.0)
        sine = jnp.sin(angles)
        sin_tab[where_rows, :] = jnp.where(lane < 32, -sine, jnp.where(lane < 64, sine, 0.0))

    def project(slot):
        block = ((y + slot // 2) % 4) * 2 + (c + slot % 2) % 2
        at = pl.ds(pl.multiple_of(block * rows, rows), rows)
        cosine, sine = cos_tab[at, :], sin_tab[at, :]

        def turn(values):
            other = jnp.where(lane < 32, pltpu.roll(values, 96, 1), pltpu.roll(values, 32, 1))
            return (values * cosine + other * sine).astype(BF16)

        own = tok[slot]
        wide = lax.dot_general(own, wq_wide[...], (((1,), (1,)), ((), ())), preferred_element_type=F32)
        for h in range(3):
            q_ref[at, h * 128 : (h + 1) * 128] = turn(wide[:, h * 128 : (h + 1) * 128])
        kv_ref[at, :] = turn(jnp.dot(own, wkv_ref[...], preferred_element_type=F32))

    project(0)
    copies[0].wait_recv()
    copies[3].start()
    copies[4].start()
    copies[1].wait_recv()
    copies[5].start()
    copies[6].start()
    copies[2].wait_recv()
    project(1)
    project(6)
    project(2)
    copies[3].wait_recv()
    copies[5].wait_recv()
    copies[7].start()
    copies[4].wait_recv()
    project(7)
    copies[6].wait_recv()
    project(3)
    project(4)
    copies[7].wait_recv()
    project(5)
    for one in copies:
        one.wait_send()


def project_tokens(hidden, gain, wq_t, wkv, freq, span_t, ctx):
    rows, width = hidden.shape
    tokens = rows * 8
    return pl.pallas_call(
        project_kernel,
        name="project_tokens",
        out_shape=(
            jax.ShapeDtypeStruct((tokens, 384), BF16),
            jax.ShapeDtypeStruct((tokens, 128), BF16),
        ),
        in_specs=[vmem()] * 5 + [smem()] * 2,
        out_specs=(vmem(), vmem()),
        scratch_shapes=[
            pltpu.VMEM((8, rows, width), BF16),
            pltpu.VMEM((384, width), BF16),
            pltpu.VMEM((tokens, 128), F32),
            pltpu.VMEM((tokens, 128), F32),
            pltpu.SemaphoreType.DMA((8,)),
            pltpu.SemaphoreType.DMA((8,)),
        ],
        compiler_params=pltpu.CompilerParams(
            collective_id=0, has_side_effects=True, vmem_limit_bytes=VMEM_BYTES
        ),
    )(hidden, gain, wq_t, wkv, freq, span_t, ctx)


KEYS = 512
NEW_KEYS = 256
TILE = 128


def attend_kernel(
    q_ref, kv_ref, cache_ref, routes_ref, gates_ref, span_ref, ctx_ref,
    attn_ref, kvx_ref,
    kv_wide, top, total, mixed,
):
    group = lax.axis_index("req")
    tokens = q_ref.shape[0]
    kv_wide[pl.ds(0, tokens), :] = kv_ref[...].astype(F32)
    scale = LOG2E / 8.0

    def fold(queries, keys, bias):
        scores = lax.dot_general(queries, keys, (((1,), (1,)), ((), ())), preferred_element_type=F32)
        scores = scores * scale + bias
        old = top[...]
        new = jnp.maximum(old, jnp.max(scores, axis=1, keepdims=True))
        probs = jnp.exp2(scores - new)
        fade = jnp.exp2(old - new)
        top[...] = new
        total[...] = total[...] * fade + jnp.sum(probs, axis=1, keepdims=True)
        mixed[...] = mixed[...] * fade + jnp.dot(probs.astype(BF16), keys, preferred_element_type=F32)

    def prompt(j, carry):
        begin, packed = carry
        length = span_ref[j, group]
        end = begin + length
        ctx = ctx_ref[group * 4 + j]

        def tile(t, _):
            first = pl.multiple_of(t * TILE, TILE)
            at = pl.ds(first, TILE)
            queries = jnp.concatenate([q_ref[at, h * 128 : (h + 1) * 128] for h in range(3)], axis=0)
            top[...] = jnp.full_like(top, -3e38)
            total[...] = jnp.zeros_like(total)
            mixed[...] = jnp.zeros_like(mixed)

            def old_keys(i, _):
                keys = cache_ref[j, pl.ds(pl.multiple_of(i * KEYS, KEYS), KEYS), :]
                col = lax.broadcasted_iota(jnp.int32, (1, KEYS), 1) + i * KEYS
                fold(queries, keys, jnp.where(col < ctx, 0.0, -1e30))
                return 0

            lax.fori_loop(0, (ctx + KEYS - 1) // KEYS, old_keys, 0)

            def new_keys(i, _):
                keys = kv_ref[pl.ds(pl.multiple_of(i * NEW_KEYS, NEW_KEYS), NEW_KEYS), :]
                col = lax.broadcasted_iota(jnp.int32, (3 * TILE, NEW_KEYS), 1) + i * NEW_KEYS
                row = lax.broadcasted_iota(jnp.int32, (3 * TILE, NEW_KEYS), 0) % TILE + first
                fold(queries, keys, jnp.where((col >= begin) & (col <= row), 0.0, -1e30))
                return 0

            lax.fori_loop(begin // NEW_KEYS, (first + TILE - 1) // NEW_KEYS + 1, new_keys, 0)
            out = mixed[...] / total[...]
            side = jnp.concatenate([out[h * TILE : (h + 1) * TILE, 64:] for h in range(3)], axis=1)
            row = lax.broadcasted_iota(jnp.int32, side.shape, 0) + first
            mine = (row >= begin) & (row < end)
            attn_ref[at, :] = jnp.where(mine, side, attn_ref[at, :].astype(F32)).astype(BF16)
            return 0

        lax.fori_loop(begin // TILE, (end + TILE - 1) // TILE, tile, 0)

        def pack(i, _):
            dst = pl.ds(pl.multiple_of(packed + i * 16, 16), 16)
            kvx_ref[dst, :] = kv_wide[pl.ds(begin + i * 16, 16), :].astype(BF16)
            return 0

        chunks = (length + 15) // 16
        lax.fori_loop(0, chunks, pack, 0)
        return end, packed + chunks * 16

    kv_wide[pl.ds(tokens, 16), :] = jnp.zeros((16, 128), F32)
    kvx_ref[...] = jnp.zeros_like(kvx_ref)
    attn_ref[...] = jnp.zeros_like(attn_ref)
    lax.fori_loop(0, 4, prompt, (0, 0))
    expert = lax.broadcasted_iota(jnp.int32, (32, 128), 0)
    gates = jnp.zeros((32, 128), F32)
    for k in range(8):
        hit = routes_ref[k : k + 1, :] == expert
        gates = gates + jnp.where(hit, gates_ref[k : k + 1, :].astype(F32), 0.0)
    kvx_ref[pl.ds(1088, 32), :] = gates.astype(BF16)


def attend(q, kv, cache, routes_t, gates_t, span_t, ctx):
    tokens = q.shape[0]
    return pl.pallas_call(
        attend_kernel,
        name="attend",
        out_shape=(
            jax.ShapeDtypeStruct((tokens, 192), BF16),
            jax.ShapeDtypeStruct((1152, 128), BF16),
        ),
        in_specs=[vmem()] * 5 + [smem()] * 2,
        out_specs=(vmem(), vmem()),
        scratch_shapes=[
            pltpu.VMEM((tokens + 16, 128), F32),
            pltpu.VMEM((3 * TILE, 1), F32),
            pltpu.VMEM((3 * TILE, 1), F32),
            pltpu.VMEM((3 * TILE, 128), F32),
        ],
        compiler_params=pltpu.CompilerParams(vmem_limit_bytes=VMEM_BYTES),
    )(q, kv, cache, routes_t, gates_t, span_t, ctx)


def body(
    hidden_in, attn_gain, w_query, keyvalue_weight, w_out, cache_kv, ctx_len, span_len,
    ffn_gain, routes, gate_weights, w_gate_up, w_down, req_prompt, cache_slot,
):
    rows_dev, width = hidden_in.shape
    prompts_dev = cache_kv.shape[0]
    span_t = span_len.T
    lane = jnp.arange(128)
    freq = (ROPE_BASE ** (-2.0 * (lane % 32).astype(F32) / 64.0))[None, :]
    q, kv = project_tokens(
        hidden_in, attn_gain[None, :], w_query.T, keyvalue_weight.reshape(width, 128), freq, span_t, ctx_len
    )
    attn, kvx = attend(
        q, kv, cache_kv.reshape(prompts_dev, -1, 128), routes.T, gate_weights.T, span_t, ctx_len
    )
    tok_dev = q.shape[0]
    span_most = tok_dev // 2
    projected = lax.psum_scatter(
        jnp.dot(attn, w_out, preferred_element_type=F32), "head", scatter_dimension=0, tiled=True
    )
    resid = hidden_in.astype(F32) + projected
    expert_in = rms(resid, ffn_gain).astype(BF16)
    n_owners = lax.axis_size("req")
    local_experts = w_gate_up.shape[0]
    experts_all = local_experts * n_owners
    slots_all = experts_all * CAP
    pair_expert = routes.reshape(-1)
    onehot = (pair_expert[:, None] == jnp.arange(experts_all)[None, :]).astype(jnp.int32)
    ranks = jnp.cumsum(onehot, axis=0) - onehot
    slot_pos = jnp.sum(ranks * onehot, axis=1)
    slot_ids = pair_expert * CAP + slot_pos
    table = jnp.arange(slots_all)[:, None] == slot_ids[None, :]
    topk = routes.shape[1]
    send_map = jnp.any(table.reshape(slots_all, rows_dev, topk), axis=-1).astype(BF16)
    gate_flat = gate_weights.reshape(-1).astype(F32)
    combine_map = jnp.sum(
        jnp.where(table, gate_flat[None, :], 0.0).reshape(slots_all, rows_dev, topk), axis=-1
    ).astype(BF16)
    buffer = jnp.dot(send_map, expert_in, preferred_element_type=F32).astype(BF16)
    ff_width = w_down.shape[1]
    received = lax.all_to_all(
        buffer.reshape(experts_all, CAP, width), "req", split_axis=0, concat_axis=0, tiled=True
    )
    slot_count = received.shape[1]
    blocks = received.reshape(n_owners, local_experts, slot_count, width)
    both = jnp.einsum("secd,edf->secf", blocks, w_gate_up, preferred_element_type=F32)
    act = (jax.nn.silu(both[..., :ff_width]) * both[..., ff_width:]).astype(BF16)
    outputs = jnp.einsum("secf,efd->secd", act, w_down, preferred_element_type=F32).astype(BF16)
    returned = lax.all_to_all(
        outputs.reshape(received.shape), "req", split_axis=0, concat_axis=0, tiled=True
    )
    moe_sum = jnp.einsum(
        "sr,sd->rd", combine_map, returned.reshape(slots_all, width), preferred_element_type=F32
    )
    layer_out = (resid + moe_sum).astype(BF16)
    all_kv = lax.all_gather(kvx[:1088], "req", axis=0, tiled=True)
    padded = (span_len + 15) // 16 * 16
    starts_table = jnp.cumsum(padded, axis=1) - padded
    starts_table = (starts_table + jnp.arange(16)[:, None] * 1088).reshape(-1)
    lengths_table = span_len.reshape(-1)
    slot_of = cache_slot[:, None] == jnp.arange(18)[None, :]
    prompt = jnp.sum(jnp.where(slot_of, req_prompt[:, None], 0), axis=0)
    pick = prompt[:, None] == jnp.arange(64)[None, :]
    req_start = jnp.sum(jnp.where(pick, starts_table[None, :], 0), axis=1)
    req_length = jnp.sum(jnp.where(pick, lengths_table[None, :], 0), axis=1)
    cache = slot_rows(all_kv, req_start, req_length)
    return (layer_out, cache.reshape(18, span_most, 1, 128))


def slot_kernel(start_ref, length_ref, all_ref, out_ref):
    s = pl.program_id(0)
    first = pl.multiple_of(start_ref[s], 16)

    @pl.loop(0, 32)
    def _(i):
        rows = all_ref[pl.ds(pl.multiple_of(jnp.minimum(first + i * 16, 17408 - 16), 16), 16), :]
        at = lax.broadcasted_iota(jnp.int32, rows.shape, 0) + i * 16
        kept = jnp.where(at < length_ref[s], rows.astype(F32), 0.0).astype(BF16)
        out_ref[0, pl.ds(pl.multiple_of(i * 16, 16), 16), :] = kept


def slot_rows(all_kv, start, length):
    return pl.pallas_call(
        slot_kernel,
        name="slot_rows",
        grid_spec=pltpu.PrefetchScalarGridSpec(
            num_scalar_prefetch=2,
            grid=(18,),
            in_specs=[pl.BlockSpec(all_kv.shape, lambda s, a, b: (0, 0), pipeline_mode=pl.Buffered(1))],
            out_specs=pl.BlockSpec((1, 512, 128), lambda s, a, b: (s, 0, 0)),
        ),
        out_shape=jax.ShapeDtypeStruct((18, 512, 128), BF16),
        compiler_params=pltpu.CompilerParams(vmem_limit_bytes=VMEM_BYTES),
    )(start, length, all_kv)


def solution(mesh):
    placed = (
        P(("req", "head"), None),
        P(),
        P(None, "head"),
        P(None, "head", None),
        P("head", None),
        P("req", None, "head", None),
        P(),
        P(),
        P(),
        P(("req", "head"), None),
        P(("req", "head"), None),
        P("req", None, None),
        P("req", None, None),
        P("req"),
        P("req"),
    )
    return jax.shard_map(
        body,
        mesh=mesh,
        in_specs=placed,
        out_specs=(P(("req", "head"), None), P("req", None, "head", None)),
        check_vma=False,
    )
```

profile of v0, /device:TPU:108, one launch (start us, length us, event | category | flops | bytes accessed | tf_op | source)
XLA Modules:
  0.0 330.5 jit_solution(16084818581277677659)
XLA Ops:
  8.6 1.3 broadcast_in_dim.62.gain_ref
  9.9 22.6 %project_tokens.1 = (bf16[1024,384]{1,0:T(8,128)(2,1)}, bf16[1024,128]{1,0:T(8,128)(2,1)}) custom-call(bf16[128,1536]{1,0:T(8,128)(2,1)} %hidden_ref.1, f32[1,1536]{1,0:T(1,128)} %broadcast_in_dim.62.gain_ref, bf16[192,1536]{1,0:T(8,128)(2,1)} %bitcast.56, bf16[1536,128]{1,0:T(8,128)(2,1)} %bitcast.58, f32[1,128]{1,0:T(1,128)} %fusion.26.freq_ref, ...), custom_call_target="tpu_custom_call" | custom-call | tf_op jit(solution)/shard_map/project_tokens/pallas_call | solution.py:150
  32.5 39.1 %attend.1 = (bf16[1024,192]{1,0:T(8,128)(2,1)}, bf16[1152,128]{1,0:T(8,128)(2,1)}) custom-call(bf16[1024,384]{1,0:T(8,128)(2,1)} %get-tuple-element.6.q_ref, bf16[1024,128]{1,0:T(8,128)(2,1)} %get-tuple-element.7.kv_ref, bf16[4,2048,128]{2,1,0:T(8,128)(2,1)} %bitcast.55, s32[8,128]{1,0:T(8,128)} %bitcast.61, bf16[8,128]{1,0:T(8,128)(2,1)} %bitcast.63, ...), custom_call_target="tpu_custom_call" | custom-call | tf_op jit(solution)/shard_map/attend/pallas_call | solution.py:261
  71.5 4.7 %fusion.28 = f32[1024,1536]{1,0:T(8,128)} fusion(bf16[1024,192]{1,0:T(8,128)(2,1)} %get-tuple-element.8, bf16[192,1536]{1,0:T(8,128)(2,1)S(1)} %copy-done.2), kind=kOutput, calls=%fused_computation.51 | convolution fusion | flops 603979776 | bytes 7274496 | tf_op jit(solution)/shard_map/dot_general | solution.py:298
  78.6 1.5 eq.69
  80.7 17.5 %reduce-window.6 = s32[32,8,128]{2,1,0:T(8,128)} reduce-window(s32[32,8,128]{2,1,0:T(8,128)} %fusion.20, s32[]{:T(128)} %constant.50.clone.1), window={size=1x1x128 pad=0_0x0_0x127_0}, to_apply=%region_1.2 | reduce-window | flops 4161536 | bytes 262148 | tf_op jit(solution)/shard_map/reduce-window
  98.2 1.7 slice.20
  106.3 6.2 %fusion.2 = pred[1536,128]{1,0:T(8,128)(4,1)} fusion(s32[128,8]{0,1:T(8,128)S(1)} %multiply_add_fusion), kind=kLoop, calls=%fused_computation.5 | loop fusion | flops 2949120 | bytes 200704 | tf_op jit(solution)/shard_map/reduce_or | solution.py:313
  112.6 15.7 %reduce-scatter.2.cloned.1.call-done = f32[128,1536]{1,0:T(8,128)} async-done(((f32[1024,1536]{1,0:T(8,128)}), f32[128,1536]{1,0:T(8,128)}) %reduce-scatter.2.cloned.1.call-update) | async-done | bytes 786448 | tf_op jit(solution)/shard_map/reduce_scatter | solution.py:297
  128.3 1.3 multiply_reduce_fusion
  129.6 4.9 %convolution_convert_fusion = bf16[1536,1536]{1,0:T(8,128)(2,1)} fusion(pred[1536,128]{1,0:T(8,128)(4,1)} %fusion.2, f32[1536]{0:T(1024)} %param.23, f32[128]{0:T(128)S(1)} %add_rsqrt_fusion, f32[128,1536]{1,0:T(8,128)} %reduce-scatter.2.cloned.1.call-done, bf16[128,1536]{1,0:T(8,128)(2,1)S(1)} %copy-done.1), kind=kOutput, calls=%fused_computation | convolution fusion | flops 607322112 | bytes 6101504 | tf_op jit(solution)/shard_map/dot_general | solution.py:318
  134.5 7.2 %all-to-all-start = ((bf16[32,48,1536]{2,1,0:T(8,128)(2,1)}), bf16[32,48,1536]{2,1,0:T(8,128)(2,1)}, u32[]{:S(2)}, u32[]{:S(2)}) async-start(bf16[32,48,1536]{2,1,0:T(8,128)(2,1)} %bitcast.52), calls=%async_computation.1 | async-start | bytes 9437184 | tf_op jit(solution)/shard_map/all_to_all | solution.py:320
  141.7 1.7 slice.19
  143.4 70.5 %all-to-all-done = bf16[32,48,1536]{2,1,0:T(8,128)(2,1)} async-done(((bf16[32,48,1536]{2,1,0:T(8,128)(2,1)}), bf16[32,48,1536]{2,1,0:T(8,128)(2,1)}, u32[]{:S(2)}, u32[]{:S(2)}) %all-to-all-start) | async-done | bytes 4718624 | tf_op jit(solution)/shard_map/all_to_all | solution.py:320
  213.9 8.5 %fusion.6 = f32[16,2,48,1024]{3,2,0,1:T(8,128)S(1)} fusion(bf16[2,1536,1024]{2,1,0:T(8,128)(2,1)} %param.26, bf16[16,2,48,1536]{3,2,1,0:T(8,128)(2,1)} %bitcast.9), kind=kOutput, calls=%fused_computation.11 | convolution fusion | flops 4831838208 | bytes 17301504 | tf_op jit(solution)/shard_map/secd,edf->secf/dot_general | solution.py:325
  222.5 2.9 convert_bitcast_fusion
  225.4 2.5 copy.52
  227.9 15.0 %all-to-all-start.1 = ((bf16[32,48,1536]{2,1,0:T(8,128)(2,1)}), bf16[32,48,1536]{2,1,0:T(8,128)(2,1)}, u32[]{:S(2)}, u32[]{:S(2)}) async-start(bf16[32,48,1536]{2,1,0:T(8,128)(2,1)} %bitcast.53), calls=%async_computation.2 | async-start | bytes 9437184 | tf_op jit(solution)/shard_map/all_to_all | solution.py:328
  246.7 1.3 copy.53
  250.2 1.4 select_reduce_fusion.1
  251.6 9.6 %select_reduce_fusion = bf16[1536,128]{1,0:T(8,128)(2,1)} fusion(f32[128,8]{0,1:T(8,128)} %convert_element_type.53, s32[128,8]{0,1:T(8,128)S(1)} %multiply_add_fusion), kind=kLoop, calls=%fused_computation.3 | loop fusion | flops 4521984 | bytes 401408 | tf_op jit(solution)/shard_map/reduce_sum | solution.py:315
  261.2 11.7 %slot_rows.1 = bf16[18,512,128]{2,1,0:T(8,128)(2,1)} custom-call(s32[18]{0:T(128)} %get-tuple-element.19.start_ref, s32[18]{0:T(128)} %get-tuple-element.18.length_ref, bf16[17408,128]{1,0:T(8,128)(2,1)} %all-gather.2.cloned.1.call-done.all_ref), custom_call_target="tpu_custom_call" | custom-call | tf_op jit(solution)/shard_map/slot_rows/pallas_call | solution.py:362
  272.9 46.0 %all-to-all-done.1 = bf16[32,48,1536]{2,1,0:T(8,128)(2,1)} async-done(((bf16[32,48,1536]{2,1,0:T(8,128)(2,1)}), bf16[32,48,1536]{2,1,0:T(8,128)(2,1)}, u32[]{:S(2)}, u32[]{:S(2)}) %all-to-all-start.1) | async-done | bytes 4718624 | tf_op jit(solution)/shard_map/all_to_all | solution.py:328
  318.8 4.2 %fusion.11 = bf16[128,1536]{1,0:T(8,128)(2,1)} fusion(bf16[1536,1536]{1,0:T(8,128)(2,1)} %bitcast.17, bf16[1536,128]{1,0:T(8,128)(2,1)} %select_reduce_fusion, f32[128,1536]{1,0:T(8,128)} %reduce-scatter.2.cloned.1.call-done, bf16[128,1536]{1,0:T(8,128)(2,1)S(1)} %copy-done.1), kind=kOutput, calls=%fused_computation.13 | convolution fusion | flops 604766208 | bytes 6684672 | tf_op jit(solution)/shard_map/sr,sd->rd/dot_general | solution.py:331
  (40 shorter events, 16.1 us)
Async XLA Ops:
  8.0 214.5 %copy-start = (bf16[2,512,1536]{2,1,0:T(8,128)(2,1)S(1)}, bf16[2,512,1536]{2,1,0:T(8,128)(2,1)}, u32[]{:S(2)}) copy-start(bf16[2,512,1536]{2,1,0:T(8,128)(2,1)} %param.27) | copy-start | bytes 9437188
  8.0 120.3 %reduce-scatter.2.cloned.1.call-start = ((), (), s32[]{:S(2)}) async-start(), calls=%async_computation.3 | async-start | bytes 7077888 | tf_op jit(solution)/shard_map/reduce_scatter | solution.py:297
  8.1 63.5 %copy-start.2 = (bf16[192,1536]{1,0:T(8,128)(2,1)S(1)}, bf16[192,1536]{1,0:T(8,128)(2,1)}, u32[]{:S(2)}) copy-start(bf16[192,1536]{1,0:T(8,128)(2,1)} %param.19) | copy-start | bytes 1769476
  76.2 0.7 copy-start.4
  76.2 52.1 %copy-start.1 = (bf16[128,1536]{1,0:T(8,128)(2,1)S(1)}, bf16[128,1536]{1,0:T(8,128)(2,1)}, u32[]{:S(2)}) copy-start(bf16[128,1536]{1,0:T(8,128)(2,1)} %hidden_ref.1) | copy-start | bytes 1179652
  134.5 79.4 %all-to-all-start = ((bf16[32,48,1536]{2,1,0:T(8,128)(2,1)}), bf16[32,48,1536]{2,1,0:T(8,128)(2,1)}, u32[]{:S(2)}, u32[]{:S(2)}) async-start(bf16[32,48,1536]{2,1,0:T(8,128)(2,1)} %bitcast.52), calls=%async_computation.1 | async-start | bytes 9437184 | tf_op jit(solution)/shard_map/all_to_all | solution.py:320
  141.7 119.5 %all-gather.2.cloned.1.call-start = ((), (), s32[]{:S(2)}) async-start(), calls=%async_computation.4 | async-start | bytes 4734976 | tf_op jit(solution)/shard_map/all_gather | solution.py:335
  227.9 15.0 %copy-start.5 = (bf16[128,8]{0,1:T(8,128)(2,1)S(1)}, bf16[128,8]{0,1:T(8,128)(2,1)}, u32[]{:S(2)}) copy-start(bf16[128,8]{0,1:T(8,128)(2,1)} %param.25) | copy-start | bytes 6148
  227.9 15.6 %copy-start.3 = (s32[16,4]{0,1:T(4,128)S(1)}, s32[16,4]{0,1:T(4,128)}, u32[]{:S(2)}) copy-start(s32[16,4]{0,1:T(4,128)} %param.22) | copy-start | bytes 772
  227.9 90.9 %all-to-all-start.1 = ((bf16[32,48,1536]{2,1,0:T(8,128)(2,1)}), bf16[32,48,1536]{2,1,0:T(8,128)(2,1)}, u32[]{:S(2)}, u32[]{:S(2)}) async-start(bf16[32,48,1536]{2,1,0:T(8,128)(2,1)} %bitcast.53), calls=%async_computation.2 | async-start | bytes 9437184 | tf_op jit(solution)/shard_map/all_to_all | solution.py:328
Sparse Core Ops, SparseCore 0:
  76.4 51.8 reduce-scatter.1
Sparse Core Ops, SparseCore 1:
  144.9 97.4 all-gather.1
where the time goes:
time: 332 us; the launch traced here: 330 us
  waiting for transfers between devices  132 us (40%)
  Pallas kernels  73.3 us (22%)
  other arithmetic  44.2 us (13%)
  matrix products  25.2 us (8%)
  starting transfers between devices  22.2 us (7%)
  local copies, waits for them, and re-layouts  17.8 us (5%)
  between operations  15.6 us (5%)
    all_to_all x1, waiting for transfers between devices, body(): lax.all_to_all(buffer.reshape(experts_all, CAP, width), 'req', split_axis...  70.5 us
    all_to_all x1, waiting for transfers between devices, body(): lax.all_to_all(outputs.reshape(received.shape), 'req', split_axis=0, conc...  46 us
    pallas_call x1, Pallas kernels, attend(): pl.pallas_call(attend_kernel, name='attend', out_shape=(jax.ShapeDtypeStr...  39.1 us
    pallas_call x1, Pallas kernels, project_tokens(): pl.pallas_call(project_kernel, name='project_tokens', out_shape=(jax.Shap...  22.6 us
    another operation x3, other arithmetic  18.5 us
    reduce_scatter x1, waiting for transfers between devices, body(): lax.psum_scatter(jnp.dot(attn, w_out, preferred_element_type=F32), 'head'...  15.7 us
    all_to_all x1, starting transfers between devices, body(): lax.all_to_all(outputs.reshape(received.shape), 'req', split_axis=0, conc...  15 us
    pallas_call x1, Pallas kernels, slot_rows(): pl.pallas_call(slot_kernel, name='slot_rows', grid_spec=pltpu.PrefetchSca...  11.7 us
  transfers between devices with their start and end apart: 4, of which 3 were waited for; matrix products, arithmetic and copies ran while one was open for 21% of the time, Pallas kernels for 4%

commit v1 on v0

--- a/solution.py
+++ b/solution.py
@@ -15,6 +15,8 @@
 F32 = jnp.float32
 BF16 = jnp.bfloat16
 VMEM_BYTES = 60 * 1024 * 1024
+KV_ROWS = 1152
+GATE_ROW = 1088
 
 
 def vmem():
@@ -176,8 +178,8 @@
 
 
 def attend_kernel(
-    q_ref, kv_ref, cache_ref, routes_ref, gates_ref, span_ref, ctx_ref,
-    attn_ref, kvx_ref,
+    q_ref, kv_ref, cache_ref, routes_ref, gates_ref, span_ref, ctx_ref, prompt_ref, place_ref,
+    attn_ref, kvx_ref, place_rows_ref,
     kv_wide, top, total, mixed,
 ):
     group = lax.axis_index("req")
@@ -253,20 +255,32 @@
     for k in range(8):
         hit = routes_ref[k : k + 1, :] == expert
         gates = gates + jnp.where(hit, gates_ref[k : k + 1, :].astype(F32), 0.0)
-    kvx_ref[pl.ds(1088, 32), :] = gates.astype(BF16)
-
-
-def attend(q, kv, cache, routes_t, gates_t, span_t, ctx):
+    kvx_ref[pl.ds(GATE_ROW, 32), :] = gates.astype(BF16)
+
+    x, z = group // 4, group % 4
+
+    @pl.loop(0, 18)
+    def _(i):
+        asked, member = prompt_ref[i] // 4, prompt_ref[i] % 4
+        first = ((asked // 4 - x + 4) % 4 * 4 + (asked % 4 - z + 4) % 4) * KV_ROWS
+        for j in range(3):
+            first = first + jnp.where(j < member, (span_ref[j, asked] + 15) // 16 * 16, 0)
+        place_rows_ref[0, place_ref[i]] = first // 16
+        place_rows_ref[1, place_ref[i]] = span_ref[member, asked]
+
+
+def attend(q, kv, cache, routes_t, gates_t, span_t, ctx, req_prompt, cache_slot):
     tokens = q.shape[0]
     return pl.pallas_call(
         attend_kernel,
         name="attend",
         out_shape=(
             jax.ShapeDtypeStruct((tokens, 192), BF16),
-            jax.ShapeDtypeStruct((1152, 128), BF16),
+            jax.ShapeDtypeStruct((KV_ROWS, 128), BF16),
+            jax.ShapeDtypeStruct((2, 18), jnp.int32),
         ),
-        in_specs=[vmem()] * 5 + [smem()] * 2,
-        out_specs=(vmem(), vmem()),
+        in_specs=[vmem()] * 5 + [smem()] * 4,
+        out_specs=(vmem(), vmem(), smem()),
         scratch_shapes=[
             pltpu.VMEM((tokens + 16, 128), F32),
             pltpu.VMEM((3 * TILE, 1), F32),
@@ -274,14 +288,473 @@
             pltpu.VMEM((3 * TILE, 128), F32),
         ],
         compiler_params=pltpu.CompilerParams(vmem_limit_bytes=VMEM_BYTES),
-    )(q, kv, cache, routes_t, gates_t, span_t, ctx)
+    )(q, kv, cache, routes_t, gates_t, span_t, ctx, req_prompt, cache_slot)
+
+
+GROUPS = (
+    ((0, 0), (0, 1), (0, 3), (1, 0), (3, 0)),
+    ((0, 2), (2, 0), (1, 1), (1, 3), (3, 1), (3, 3)),
+    ((2, 2), (2, 1), (2, 3), (1, 2), (3, 2)),
+)
+
+
+def slot_of(which, first, second):
+    return first * 4 + second if which == 0 else second * 4 + first
+
+
+class Line:
+    def __init__(self, make, ssem, rsem, base, outs, passes):
+        self.copies = [
+            make(src, dst, ssem.at[base + i], rsem.at[base + i], to)
+            for i, (src, dst, to) in enumerate(outs + passes)
+        ]
+
+    def out(self):
+        self.copies[0].start()
+        self.copies[1].start()
+
+    def forward(self):
+        self.copies[0].wait_recv()
+        self.copies[2].start()
+        self.copies[1].wait_recv()
+        self.copies[3].start()
+
+    def finish(self):
+        self.copies[2].wait_recv()
+        self.copies[3].wait_recv()
+
+    def drain(self):
+        for one in self.copies:
+            one.wait_send()
+
+
+def remote(axis):
+    def make(src, dst, send, recv, to):
+        return pltpu.make_async_remote_copy(
+            src_ref=src, dst_ref=dst, send_sem=send, recv_sem=recv, device_id={axis: to}, device_id_type=MESH
+        )
+
+    return make
+
+
+def gather_lines(buf, rows, ssem, rsem, ring):
+    half, quarter = rows // 2, rows // 4
+    lines = []
+    for which in (0, 1):
+        plus, minus = ring[which]
+        plus2, minus2 = ring[1 - which]
+        low = which * half
+
+        def part(first, second, piece, which=which, low=low):
+            row, count = {"all": (low, half), "a": (low, quarter), "b": (low + quarter, quarter)}[piece]
+            return buf(slot_of(which, first, second), row, count)
+
+        def along(base, at, p, m, part=part):
+            return Line(
+                remote("req"), ssem, rsem, base,
+                [(part(*at(0), "all"), part(*at(3), "all"), p), (part(*at(0), "all"), part(*at(1), "all"), m)],
+                [(part(*at(3), "a"), part(*at(2), "a"), p), (part(*at(1), "b"), part(*at(2), "b"), m)],
+            )
+
+        these = [along(which * 20, lambda k: (k, 0), plus, minus)]
+        for i in range(4):
+            these.append(along(which * 20 + 4 + 4 * i, lambda k, i=i: (i, k), plus2, minus2))
+        lines.append(these)
+    return lines
+
+
+def gather_steps(lines):
+    def both(*steps):
+        for one in lines:
+            for index, name in steps:
+                getattr(one[index], name)()
+
+    return [
+        lambda: both((0, "out"), (1, "out")),
+        lambda: both((0, "forward"), (4, "out"), (2, "out")),
+        lambda: both((1, "forward")),
+        lambda: both((0, "finish"), (3, "out")),
+        lambda: both((4, "forward"), (2, "forward")),
+        lambda: both((1, "finish")),
+        lambda: both((3, "forward")),
+        lambda: both((4, "finish"), (2, "finish")),
+        lambda: both((3, "finish")),
+        lambda: [line.drain() for one in lines for line in one],
+    ]
+
+
+def finish_kernel(
+    attn_ref, wout_ref, hidden_ref, gain_ref, kvx_ref, place_ref, wgu_hbm, wd_hbm,
+    out_ref, cache_hbm,
+    wgu, wd, part, pin, head_half, head_full, resid, kvall, rows_in, sums, red_half, red_full,
+    gates, ranks, picked, acts, outs, staged,
+    wsem, csem, hssem, hrsem, kssem, krsem, assem, arsem, rssem, rrsem,
+):
+    width = hidden_ref.shape[1]
+    r = lax.axis_index("req")
+    x, z = r // 4, r % 4
+    xp, xm = ((x + 1) % 4) * 4 + z, ((x + 3) % 4) * 4 + z
+    zp, zm = x * 4 + (z + 1) % 4, x * 4 + (z + 3) % 4
+    ring = ((xp, xm), (zp, zm))
+    y, c, partner, up, down = head_neighbours()
+    wait_all = greet(
+        [("head", partner), ("head", up), ("head", down), ("req", xp), ("req", xm), ("req", zp), ("req", zm)]
+    )
+    loads = [
+        pltpu.make_async_copy(wgu_hbm, wgu, wsem.at[0]),
+        pltpu.make_async_copy(wd_hbm, wd, wsem.at[1]),
+        pltpu.make_async_copy(kvx_ref, kvall.at[pl.ds(0, KV_ROWS), :], wsem.at[2]),
+    ]
+    loads[2].start()
+    for one in loads[:2]:
+        one.start()
+    kvall[pl.ds(16 * KV_ROWS, 512), :] = jnp.zeros((512, 128), BF16)
+    loads[2].wait()
+    wait_all()
+
+    kv_lines = gather_lines(
+        lambda slot, row, count: kvall.at[pl.ds(slot * KV_ROWS + row, count), :], KV_ROWS, kssem, krsem, ring
+    )
+    kv_steps = gather_steps(kv_lines)
+    row_lines = gather_lines(
+        lambda slot, row, count: rows_in.at[slot, pl.ds(row, count), :], 128, assem, arsem, ring
+    )
+    row_steps = gather_steps(row_lines)
+    kv_steps[0]()
+
+    def project(dy, dc, store, extra=()):
+        target = ((y + dy) % 4) * 2 + (c + dc) % 2
+        own = attn_ref[pl.ds(pl.multiple_of(target * 128, 128), 128), :]
+
+        @pl.loop(0, width // 256)
+        def _(n):
+            cols = pl.ds(pl.multiple_of(n * 256, 256), 256)
+            total = jnp.dot(own, wout_ref[:, cols], preferred_element_type=F32)
+            store(cols, total)
+
+    def into(index):
+        def store(cols, total):
+            part[index, :, cols] = total.astype(BF16)
+
+        return store
+
+    make = remote("head")
+    low, high = pl.ds(0, 64), pl.ds(64, 64)
+    to_partner = {
+        dy: make(part.at[2 * dy + 1], pin.at[dy], hssem.at[dy], hrsem.at[dy], partner) for dy in range(4)
+    }
+    halves = [
+        make(part.at[4, low], head_half.at[0], hssem.at[4], hrsem.at[4], up),
+        make(part.at[4, high], head_half.at[1], hssem.at[5], hrsem.at[5], down),
+    ]
+    fulls = [
+        make(part.at[2], head_full.at[0], hssem.at[6], hrsem.at[6], up),
+        make(part.at[6], head_full.at[1], hssem.at[7], hrsem.at[7], down),
+    ]
+    for dy in (2, 1, 3, 0):
+        project(dy, 1, into(2 * dy + 1))
+        to_partner[dy].start()
+
+    to_partner[2].wait_recv()
+
+    def store_two(cols, total):
+        part[4, :, cols] = (total + pin[2, :, cols].astype(F32)).astype(BF16)
+
+    project(2, 0, store_two)
+    for one in halves:
+        one.start()
+    kv_steps[1]()
+    to_partner[1].wait_recv()
+    halves[0].wait_recv()
+
+    def store_one(cols, total):
+        total = total + pin[1, :, cols].astype(F32)
+        part[2, low, cols] = (total[:64] + head_half[0, :, cols].astype(F32)).astype(BF16)
+        part[2, high, cols] = total[64:].astype(BF16)
+
+    project(1, 0, store_one)
+    fulls[0].start()
+    to_partner[3].wait_recv()
+    halves[1].wait_recv()
+
+    def store_three(cols, total):
+        total = total + pin[3, :, cols].astype(F32)
+        part[6, low, cols] = total[:64].astype(BF16)
+        part[6, high, cols] = (total[64:] + head_half[1, :, cols].astype(F32)).astype(BF16)
+
+    project(3, 0, store_three)
+    fulls[1].start()
+    kv_steps[2]()
+    kv_steps[3]()
+    kv_steps[4]()
+    to_partner[0].wait_recv()
+    fulls[0].wait_recv()
+    fulls[1].wait_recv()
+
+    def store_own(cols, total):
+        total = total + pin[0, :, cols].astype(F32) + hidden_ref[:, cols].astype(F32)
+        total = total + head_full[0, :, cols].astype(F32) + head_full[1, :, cols].astype(F32)
+        resid[:, cols] = total
+
+    project(0, 0, store_own)
+
+    @pl.loop(0, 8)
+    def _(i):
+        at = pl.ds(pl.multiple_of(i * 16, 16), 16)
+        rows_in[0, at, :] = rms(resid[at, :], gain_ref[...]).astype(BF16)
+
+    row_steps[0]()
+    kv_steps[5]()
+    kv_steps[6]()
+    kv_steps[7]()
+    kv_steps[8]()
+    expert = lax.broadcasted_iota(jnp.int32, (32, 128), 0)
+
+    @pl.loop(0, 16)
+    def _(slot):
+        table = kvall[pl.ds(pl.multiple_of(slot * KV_ROWS + GATE_ROW, 16), 32), :].astype(F32)
+        for j in range(2):
+            mine = jnp.sum(jnp.where(expert == r * 2 + j, table, 0.0), axis=0, keepdims=True)
+            gates[pl.ds(slot * 2 + j, 1), :] = mine
+
+    before = lax.broadcasted_iota(jnp.int32, (128, 128), 0) < lax.broadcasted_iota(jnp.int32, (128, 128), 1)
+    hits = jnp.where(gates[...] > 0.0, 1.0, 0.0).astype(BF16)
+    ranks[...] = jnp.dot(hits, jnp.where(before, 1.0, 0.0).astype(BF16), preferred_element_type=F32)
+
+    def chosen(slot, weighted):
+        place = lax.broadcasted_iota(jnp.int32, (CAP, 128), 0).astype(F32)
+        maps = []
+        for j in range(2):
+            gate = gates[slot * 2 + j : slot * 2 + j + 1, :]
+            value = gate if weighted else 1.0
+            hit = (ranks[slot * 2 + j : slot * 2 + j + 1, :] == place) & (gate > 0.0)
+            maps.append(jnp.where(hit, value, 0.0))
+        return jnp.concatenate(maps, axis=0).astype(BF16)
+
+    def experts(group):
+        count = len(group) * CAP
+        for k, (a, b) in enumerate(group):
+            slot = a * 4 + b
+            select = chosen(slot, False)
+
+            @pl.loop(0, width // 512)
+            def _(n, k=k, slot=slot, select=select):
+                cols = pl.ds(pl.multiple_of(n * 512, 512), 512)
+                got = jnp.dot(select, rows_in[slot, :, cols], preferred_element_type=F32).astype(BF16)
+                picked[0, pl.ds(k * CAP, CAP), cols] = got[:CAP]
+                picked[1, pl.ds(k * CAP, CAP), cols] = got[CAP:]
+
+        @pl.loop(0, 2)
+        def _(e):
+            @pl.loop(0, 2)
+            def _(n):
+                cols = pl.ds(pl.multiple_of(n * 256, 256), 256)
+                later = pl.ds(pl.multiple_of(n * 256 + 512, 256), 256)
+                own = picked[e, pl.ds(0, count), :]
+                gate = jnp.dot(own, wgu[e, :, cols], preferred_element_type=F32)
+                lift = jnp.dot(own, wgu[e, :, later], preferred_element_type=F32)
+                acts[pl.ds(0, count), cols] = (gate / (1.0 + jnp.exp(-gate)) * lift).astype(BF16)
+
+            @pl.loop(0, width // 256)
+            def _(n):
+                cols = pl.ds(pl.multiple_of(n * 256, 256), 256)
+                outs[e, pl.ds(0, count), cols] = jnp.dot(
+                    acts[pl.ds(0, count), :], wd[e, :, cols], preferred_element_type=F32
+                ).astype(BF16)
+
+        for k, (a, b) in enumerate(group):
+            slot = a * 4 + b
+            spread = chosen(slot, True)
+
+            @pl.loop(0, width // 512)
+            def _(n, k=k, slot=slot, spread=spread):
+                cols = pl.ds(pl.multiple_of(n * 512, 512), 512)
+                given = jnp.concatenate(
+                    [outs[0, pl.ds(k * CAP, CAP), cols], outs[1, pl.ds(k * CAP, CAP), cols]], axis=0
+                )
+                sums[slot, :, cols] = lax.dot_general(
+                    spread, given, (((0,), (0,)), ((), ())), preferred_element_type=F32
+                ).astype(BF16)
+
+    def add(dst, row, src, count):
+        @pl.loop(0, count // 16)
+        def _(i):
+            to = pl.ds(pl.multiple_of(row + i * 16, 16), 16)
+            at = pl.ds(pl.multiple_of(i * 16, 16), 16)
+            total = sums[dst, to, :].astype(F32)
+            for one in src:
+                total = total + one[at, :].astype(F32)
+            sums[dst, to, :] = total.astype(BF16)
+
+    def reduce_line(n, which, at, plus, minus):
+        base = which * 64
+        send = remote("req")
+
+        def piece(k, row, count):
+            return sums.at[at(k), pl.ds(base + row, count), :]
+
+        s = [rssem.at[4 * n + i] for i in range(4)]
+        g = [rrsem.at[4 * n + i] for i in range(4)]
+        copies = [
+            send(piece(2, 0, 32), red_half.at[n, 0], s[0], g[0], plus),
+            send(piece(2, 32, 32), red_half.at[n, 1], s[1], g[1], minus),
+            send(piece(1, 0, 64), red_full.at[n, 0], s[2], g[2], plus),
+            send(piece(3, 0, 64), red_full.at[n, 1], s[3], g[3], minus),
+        ]
+
+        def out():
+            copies[0].start()
+            copies[1].start()
+
+        def middle():
+            copies[0].wait_recv()
+            add(at(1), base, [red_half.at[n, 0]], 32)
+            copies[2].start()
+            copies[1].wait_recv()
+            add(at(3), base + 32, [red_half.at[n, 1]], 32)
+            copies[3].start()
+
+        def last():
+            copies[2].wait_recv()
+            copies[3].wait_recv()
+
+        def fold():
+            last()
+            add(at(0), base, [red_full.at[n, 0], red_full.at[n, 1]], 64)
+
+        def drain():
+            for one in copies:
+                one.wait_send()
+
+        return out, middle, fold, last, drain
+
+    back = []
+    for which in (0, 1):
+        plus, minus = ring[which]
+        plus2, minus2 = ring[1 - which]
+        these = [
+            reduce_line(which * 5 + i, which, lambda k, i=i, w=which: slot_of(w, i, k), plus2, minus2)
+            for i in range(4)
+        ]
+        these.append(reduce_line(which * 5 + 4, which, lambda k, w=which: slot_of(w, k, 0), plus, minus))
+        back.append(these)
+
+    def go(line, step):
+        for these in back:
+            these[line][step]()
+
+    row_steps[1]()
+    row_steps[2]()
+    for one in loads[:2]:
+        one.wait()
+    experts(GROUPS[0])
+    row_steps[3]()
+    row_steps[4]()
+
+    @pl.loop(0, 18)
+    def _(s):
+        start, length = place_ref[0, s], place_ref[1, s]
+        for i in range(4):
+            rows = kvall[pl.ds(start * 16 + i * 128, 128), :].astype(F32)
+            at = lax.broadcasted_iota(jnp.int32, (128, 128), 0) + i * 128
+            staged[s, pl.ds(i * 128, 128), :] = jnp.where(at < length, rows, 0.0).astype(BF16)
+
+    store = pltpu.make_async_copy(staged, cache_hbm, csem.at[0])
+    store.start()
+    row_steps[5]()
+    experts(GROUPS[1])
+    go(0, 0)
+    row_steps[6]()
+    row_steps[7]()
+    go(0, 1)
+    row_steps[8]()
+    experts(GROUPS[2])
+    go(2, 0)
+    go(1, 0)
+    go(3, 0)
+    go(0, 2)
+    go(2, 1)
+    go(1, 1)
+    go(3, 1)
+    go(2, 2)
+    go(4, 0)
+    go(1, 2)
+    go(3, 2)
+    go(4, 1)
+    go(4, 3)
+    for which, n in ((0, 4), (1, 9)):
+        @pl.loop(0, 4)
+        def _(i, which=which, n=n):
+            to = pl.ds(pl.multiple_of(which * 64 + i * 16, 16), 16)
+            at = pl.ds(pl.multiple_of(i * 16, 16), 16)
+            total = resid[to, :] + sums[0, to, :].astype(F32)
+            total = total + red_full[n, 0, at, :].astype(F32) + red_full[n, 1, at, :].astype(F32)
+            out_ref[to, :] = total.astype(BF16)
+
+    for dy in range(4):
+        to_partner[dy].wait_send()
+    for one in halves + fulls:
+        one.wait_send()
+    kv_steps[9]()
+    row_steps[9]()
+    for line in range(5):
+        go(line, 4)
+    store.wait()
+
+
+def finish(attn, w_out, hidden, gain, kvx, place_rows, w_gate_up, w_down):
+    rows, width = hidden.shape
+    most = max(len(group) for group in GROUPS) * CAP
+    return pl.pallas_call(
+        finish_kernel,
+        name="finish",
+        out_shape=(
+            jax.ShapeDtypeStruct((rows, width), BF16),
+            jax.ShapeDtypeStruct((18, 512, 128), BF16),
+        ),
+        in_specs=[vmem()] * 5 + [smem()] + [anyspace()] * 2,
+        out_specs=(vmem(), anyspace()),
+        scratch_shapes=[
+            pltpu.VMEM(w_gate_up.shape, BF16),
+            pltpu.VMEM(w_down.shape, BF16),
+            pltpu.VMEM((8, rows, width), BF16),
+            pltpu.VMEM((4, rows, width), BF16),
+            pltpu.VMEM((2, rows // 2, width), BF16),
+            pltpu.VMEM((2, rows, width), BF16),
+            pltpu.VMEM((rows, width), F32),
+            pltpu.VMEM((16 * KV_ROWS + 512, 128), BF16),
+            pltpu.VMEM((16, rows, width), BF16),
+            pltpu.VMEM((16, rows, width), BF16),
+            pltpu.VMEM((10, 2, rows // 4, width), BF16),
+            pltpu.VMEM((10, 2, rows // 2, width), BF16),
+            pltpu.VMEM((32, 128), F32),
+            pltpu.VMEM((32, 128), F32),
+            pltpu.VMEM((2, most, width), BF16),
+            pltpu.VMEM((most, w_down.shape[1]), BF16),
+            pltpu.VMEM((2, most, width), BF16),
+            pltpu.VMEM((18, 512, 128), BF16),
+            pltpu.SemaphoreType.DMA((3,)),
+            pltpu.SemaphoreType.DMA((1,)),
+            pltpu.SemaphoreType.DMA((8,)),
+            pltpu.SemaphoreType.DMA((8,)),
+            pltpu.SemaphoreType.DMA((40,)),
+            pltpu.SemaphoreType.DMA((40,)),
+            pltpu.SemaphoreType.DMA((40,)),
+            pltpu.SemaphoreType.DMA((40,)),
+            pltpu.SemaphoreType.DMA((40,)),
+            pltpu.SemaphoreType.DMA((40,)),
+        ],
+        compiler_params=pltpu.CompilerParams(
+            collective_id=1, has_side_effects=True, vmem_limit_bytes=VMEM_BYTES
+        ),
+    )(attn, w_out, hidden, gain, kvx, place_rows, w_gate_up, w_down)
 
 
 def body(
     hidden_in, attn_gain, w_query, keyvalue_weight, w_out, cache_kv, ctx_len, span_len,
     ffn_gain, routes, gate_weights, w_gate_up, w_down, req_prompt, cache_slot,
 ):
-    rows_dev, width = hidden_in.shape
+    width = hidden_in.shape[1]
     prompts_dev = cache_kv.shape[0]
     span_t = span_len.T
     lane = jnp.arange(128)
@@ -289,88 +762,14 @@
     q, kv = project_tokens(
         hidden_in, attn_gain[None, :], w_query.T, keyvalue_weight.reshape(width, 128), freq, span_t, ctx_len
     )
-    attn, kvx = attend(
-        q, kv, cache_kv.reshape(prompts_dev, -1, 128), routes.T, gate_weights.T, span_t, ctx_len
+    attn, kvx, place_rows = attend(
+        q, kv, cache_kv.reshape(prompts_dev, -1, 128), routes.T, gate_weights.T, span_t, ctx_len,
+        req_prompt, cache_slot,
     )
-    tok_dev = q.shape[0]
-    span_most = tok_dev // 2
-    projected = lax.psum_scatter(
-        jnp.dot(attn, w_out, preferred_element_type=F32), "head", scatter_dimension=0, tiled=True
+    layer_out, cache = finish(
+        attn, w_out, hidden_in, ffn_gain[None, :], kvx, place_rows, w_gate_up, w_down
     )
-    resid = hidden_in.astype(F32) + projected
-    expert_in = rms(resid, ffn_gain).astype(BF16)
-    n_owners = lax.axis_size("req")
-    local_experts = w_gate_up.shape[0]
-    experts_all = local_experts * n_owners
-    slots_all = experts_all * CAP
-    pair_expert = routes.reshape(-1)
-    onehot = (pair_expert[:, None] == jnp.arange(experts_all)[None, :]).astype(jnp.int32)
-    ranks = jnp.cumsum(onehot, axis=0) - onehot
-    slot_pos = jnp.sum(ranks * onehot, axis=1)
-    slot_ids = pair_expert * CAP + slot_pos
-    table = jnp.arange(slots_all)[:, None] == slot_ids[None, :]
-    topk = routes.shape[1]
-    send_map = jnp.any(table.reshape(slots_all, rows_dev, topk), axis=-1).astype(BF16)
-    gate_flat = gate_weights.reshape(-1).astype(F32)
-    combine_map = jnp.sum(
-        jnp.where(table, gate_flat[None, :], 0.0).reshape(slots_all, rows_dev, topk), axis=-1
-    ).astype(BF16)
-    buffer = jnp.dot(send_map, expert_in, preferred_element_type=F32).astype(BF16)
-    ff_width = w_down.shape[1]
-    received = lax.all_to_all(
-        buffer.reshape(experts_all, CAP, width), "req", split_axis=0, concat_axis=0, tiled=True
-    )
-    slot_count = received.shape[1]
-    blocks = received.reshape(n_owners, local_experts, slot_count, width)
-    both = jnp.einsum("secd,edf->secf", blocks, w_gate_up, preferred_element_type=F32)
-    act = (jax.nn.silu(both[..., :ff_width]) * both[..., ff_width:]).astype(BF16)
-    outputs = jnp.einsum("secf,efd->secd", act, w_down, preferred_element_type=F32).astype(BF16)
-    returned = lax.all_to_all(
-        outputs.reshape(received.shape), "req", split_axis=0, concat_axis=0, tiled=True
-    )
-    moe_sum = jnp.einsum(
-        "sr,sd->rd", combine_map, returned.reshape(slots_all, width), preferred_element_type=F32
-    )
-    layer_out = (resid + moe_sum).astype(BF16)
-    all_kv = lax.all_gather(kvx[:1088], "req", axis=0, tiled=True)
-    padded = (span_len + 15) // 16 * 16
-    starts_table = jnp.cumsum(padded, axis=1) - padded
-    starts_table = (starts_table + jnp.arange(16)[:, None] * 1088).reshape(-1)
-    lengths_table = span_len.reshape(-1)
-    slot_of = cache_slot[:, None] == jnp.arange(18)[None, :]
-    prompt = jnp.sum(jnp.where(slot_of, req_prompt[:, None], 0), axis=0)
-    pick = prompt[:, None] == jnp.arange(64)[None, :]
-    req_start = jnp.sum(jnp.where(pick, starts_table[None, :], 0), axis=1)
-    req_length = jnp.sum(jnp.where(pick, lengths_table[None, :], 0), axis=1)
-    cache = slot_rows(all_kv, req_start, req_length)
-    return (layer_out, cache.reshape(18, span_most, 1, 128))
-
-
-def slot_kernel(start_ref, length_ref, all_ref, out_ref):
-    s = pl.program_id(0)
-    first = pl.multiple_of(start_ref[s], 16)
-
-    @pl.loop(0, 32)
-    def _(i):
-        rows = all_ref[pl.ds(pl.multiple_of(jnp.minimum(first + i * 16, 17408 - 16), 16), 16), :]
-        at = lax.broadcasted_iota(jnp.int32, rows.shape, 0) + i * 16
-        kept = jnp.where(at < length_ref[s], rows.astype(F32), 0.0).astype(BF16)
-        out_ref[0, pl.ds(pl.multiple_of(i * 16, 16), 16), :] = kept
-
-
-def slot_rows(all_kv, start, length):
-    return pl.pallas_call(
-        slot_kernel,
-        name="slot_rows",
-        grid_spec=pltpu.PrefetchScalarGridSpec(
-            num_scalar_prefetch=2,
-            grid=(18,),
-            in_specs=[pl.BlockSpec(all_kv.shape, lambda s, a, b: (0, 0), pipeline_mode=pl.Buffered(1))],
-            out_specs=pl.BlockSpec((1, 512, 128), lambda s, a, b: (s, 0, 0)),
-        ),
-        out_shape=jax.ShapeDtypeStruct((18, 512, 128), BF16),
-        compiler_params=pltpu.CompilerParams(vmem_limit_bytes=VMEM_BYTES),
-    )(start, length, all_kv)
+    return (layer_out, cache.reshape(18, 512, 1, 128))
 
 
 def solution(mesh):

time: 332 us -> 193 us (0.58)
  the two profiles are of different devices: /device:TPU:108 before, /device:TPU:0 now
where the time goes in v1:
time: 193 us
  Pallas kernels  184 us (95%)
  local copies, waits for them, and re-layouts  7.62 us (4%)
    pallas_call x1, Pallas kernels, finish(): pl.pallas_call(finish_kernel, name='finish', out_shape=(jax.ShapeDtypeStr...  114 us
    pallas_call x1, Pallas kernels, attend(): pl.pallas_call(attend_kernel, name='attend', out_shape=(jax.ShapeDtypeStr...  47.6 us
    pallas_call x1, Pallas kernels, project_tokens(): pl.pallas_call(project_kernel, name='project_tokens', out_shape=(jax.Shap...  23 us
    unnamed x2, local copies, waits for them, and re-layouts  5.04 us

profile of v1, /device:TPU:0, one launch (start us, length us, event | category | flops | bytes accessed | tf_op | source)
XLA Modules:
  0.0 193.1 jit_solution(4774700010365706288)
XLA Ops:
  0.6 0.5 fusion.2.freq_ref
  1.2 1.3 broadcast_in_dim.7.gain_ref
  2.4 1.3 broadcast_in_dim.8.gain_ref
  3.7 23.0 %project_tokens.1 = (bf16[1024,384]{1,0:T(8,128)(2,1)}, bf16[1024,128]{1,0:T(8,128)(2,1)}) custom-call(bf16[128,1536]{1,0:T(8,128)(2,1)} %hidden_ref.3, f32[1,1536]{1,0:T(1,128)} %broadcast_in_dim.7.gain_ref, bf16[192,1536]{1,0:T(8,128)(2,1)} %bitcast.11, bf16[1536,128]{1,0:T(8,128)(2,1)} %bitcast.12, f32[1,128]{1,0:T(1,128)} %fusion.2.freq_ref, ...), custom_call_target="tpu_custom_call" | custom-call | tf_op jit(solution)/shard_map/project_tokens/pallas_call | solution.py:152
  26.8 47.6 %attend.1 = (bf16[1024,192]{1,0:T(8,128)(2,1)}, bf16[1152,128]{1,0:T(8,128)(2,1)}, s32[2,18]{1,0:T(2,128)}) custom-call(bf16[1024,384]{1,0:T(8,128)(2,1)} %get-tuple-element.9.q_ref, bf16[1024,128]{1,0:T(8,128)(2,1)} %get-tuple-element.10.kv_ref, bf16[4,2048,128]{2,1,0:T(8,128)(2,1)} %bitcast.10, s32[8,128]{1,0:T(8,128)} %bitcast.15, ...), custom_call_target="tpu_custom_call" | custom-call | tf_op jit(solution)/shard_map/attend/pallas_call | solution.py:274
  74.4 113.7 %finish.1 = (bf16[128,1536]{1,0:T(8,128)(2,1)}, bf16[18,512,128]{2,1,0:T(8,128)(2,1)}) custom-call(bf16[1024,192]{1,0:T(8,128)(2,1)} %get-tuple-element.11.attn_ref, bf16[192,1536]{1,0:T(8,128)(2,1)} %wout_ref.1, bf16[128,1536]{1,0:T(8,128)(2,1)} %hidden_ref.3, f32[1,1536]{1,0:T(1,128)} %broadcast_in_dim.8.gain_ref, ...), custom_call_target="tpu_custom_call" | custom-call | tf_op jit(solution)/shard_map/finish/pallas_call | solution.py:708
  188.1 1.8 copy.20
  189.9 3.3 %copy.21 = bf16[18,512,1,128]{3,1,2,0:T(8,128)(2,1)} copy(bf16[18,512,1,128]{3,1,2,0:T(8,128)(2,1)} %bitcast.9) | data formatting | bytes 4718592

commit v2 on v1

--- a/solution.py
+++ b/solution.py
@@ -172,67 +172,129 @@
     )(hidden, gain, wq_t, wkv, freq, span_t, ctx)
 
 
-KEYS = 512
-NEW_KEYS = 256
+KEYS = 256
+LONG = 4
 TILE = 128
 
 
 def attend_kernel(
     q_ref, kv_ref, cache_ref, routes_ref, gates_ref, span_ref, ctx_ref, prompt_ref, place_ref,
     attn_ref, kvx_ref, place_rows_ref,
-    kv_wide, top, total, mixed,
+    kv_wide, old_turned, new_turned, attn_turned, near, top, total, mixed,
 ):
     group = lax.axis_index("req")
     tokens = q_ref.shape[0]
     kv_wide[pl.ds(0, tokens), :] = kv_ref[...].astype(F32)
     scale = LOG2E / 8.0
 
-    def fold(queries, keys, bias):
-        scores = lax.dot_general(queries, keys, (((1,), (1,)), ((), ())), preferred_element_type=F32)
-        scores = scores * scale + bias
-        old = top[...]
-        new = jnp.maximum(old, jnp.max(scores, axis=1, keepdims=True))
-        probs = jnp.exp2(scores - new)
-        fade = jnp.exp2(old - new)
-        top[...] = new
-        total[...] = total[...] * fade + jnp.sum(probs, axis=1, keepdims=True)
-        mixed[...] = mixed[...] * fade + jnp.dot(probs.astype(BF16), keys, preferred_element_type=F32)
+    def score(queries, keys):
+        return lax.dot_general(keys, queries, (((1,), (1,)), ((), ())), preferred_element_type=F32)
+
+    def mix(scores, values):
+        probs = jnp.exp2(scores * scale - top[...])
+        total[...] += jnp.sum(probs.reshape(-1, 8, probs.shape[1]), axis=0)
+        mixed[...] += jnp.dot(values, probs.astype(BF16), preferred_element_type=F32)
+
+    def new_rows(i):
+        return kv_ref[pl.ds(pl.multiple_of(i * KEYS, KEYS), KEYS), :]
+
+    @pl.loop(0, tokens // KEYS)
+    def _(i):
+        new_turned[i] = new_rows(i).T[64:, :]
 
     def prompt(j, carry):
         begin, packed = carry
         length = span_ref[j, group]
         end = begin + length
         ctx = ctx_ref[group * 4 + j]
+        long = ctx // (LONG * KEYS)
+        whole = ctx // KEYS
+        new_first = begin // KEYS
+        most_chunks = cache_ref.shape[1] // KEYS
+
+        def old_rows(i, count):
+            return cache_ref[j, pl.ds(pl.multiple_of(i * KEYS, KEYS), count * KEYS), :]
+
+        @pl.loop(0, (ctx + KEYS - 1) // KEYS)
+        def _(i):
+            old_turned[i] = old_rows(i, 1).T[64:, :]
 
         def tile(t, _):
             first = pl.multiple_of(t * TILE, TILE)
             at = pl.ds(first, TILE)
             queries = jnp.concatenate([q_ref[at, h * 128 : (h + 1) * 128] for h in range(3)], axis=0)
-            top[...] = jnp.full_like(top, -3e38)
             total[...] = jnp.zeros_like(total)
             mixed[...] = jnp.zeros_like(mixed)
-
-            def old_keys(i, _):
-                keys = cache_ref[j, pl.ds(pl.multiple_of(i * KEYS, KEYS), KEYS), :]
-                col = lax.broadcasted_iota(jnp.int32, (1, KEYS), 1) + i * KEYS
-                fold(queries, keys, jnp.where(col < ctx, 0.0, -1e30))
-                return 0
-
-            lax.fori_loop(0, (ctx + KEYS - 1) // KEYS, old_keys, 0)
-
-            def new_keys(i, _):
-                keys = kv_ref[pl.ds(pl.multiple_of(i * NEW_KEYS, NEW_KEYS), NEW_KEYS), :]
-                col = lax.broadcasted_iota(jnp.int32, (3 * TILE, NEW_KEYS), 1) + i * NEW_KEYS
-                row = lax.broadcasted_iota(jnp.int32, (3 * TILE, NEW_KEYS), 0) % TILE + first
-                fold(queries, keys, jnp.where((col >= begin) & (col <= row), 0.0, -1e30))
-                return 0
-
-            lax.fori_loop(begin // NEW_KEYS, (first + TILE - 1) // NEW_KEYS + 1, new_keys, 0)
-            out = mixed[...] / total[...]
-            side = jnp.concatenate([out[h * TILE : (h + 1) * TILE, 64:] for h in range(3)], axis=1)
-            row = lax.broadcasted_iota(jnp.int32, side.shape, 0) + first
+            lane_row = lax.broadcasted_iota(jnp.int32, (1, 3 * TILE), 1) % TILE + first
+            own_lane = (lane_row >= begin) & (lane_row < end)
+            new_last = (first + TILE - 1) // KEYS
+
+            def new_scores(i):
+                scores = score(queries, new_rows(i))
+                key = lax.broadcasted_iota(jnp.int32, (KEYS, TILE), 0) + i * KEYS
+                row = lax.broadcasted_iota(jnp.int32, (KEYS, TILE), 1) + first
+                bias = jnp.where((key >= begin) & (key <= row), 0.0, -1e30)
+                return scores + jnp.concatenate([bias] * 3, axis=1)
+
+            def last_old():
+                scores = score(queries, old_rows(jnp.minimum(whole, most_chunks - 1), 1))
+                key = lax.broadcasted_iota(jnp.int32, scores.shape, 0)
+                return jnp.where(key < ctx - whole * KEYS, scores, -1e30)
+
+            near[...] = new_scores(new_last)
+            top[...] = jnp.where(own_lane, jnp.max(near[...], axis=0, keepdims=True) * scale, 1e30)
+            mix(near[...], new_turned[new_last])
+
+            @pl.loop(new_first, new_last)
+            def _(i):
+                mix(new_scores(i), new_turned[i])
+
+            @pl.loop(0, long)
+            def _(i):
+                values = jnp.concatenate([old_turned[i * LONG + k] for k in range(LONG)], axis=1)
+                mix(score(queries, old_rows(i * LONG, LONG)), values)
+
+            @pl.loop(long * LONG, whole)
+            def _(i):
+                mix(score(queries, old_rows(i, 1)), old_turned[i])
+
+            @pl.when(ctx > whole * KEYS)
+            def _():
+                mix(last_old(), old_turned[whole])
+
+            @pl.when(jnp.max(jnp.where(own_lane, jnp.max(total[...], axis=0, keepdims=True), 0.0)) > 2.0**64)
+            def _():
+                def higher(scores):
+                    return jnp.max(scores, axis=0, keepdims=True)
+
+                most = higher(near[...])
+                most = lax.fori_loop(new_first, new_last, lambda i, m: jnp.maximum(m, higher(new_scores(i))), most)
+                most = lax.fori_loop(
+                    0, whole, lambda i, m: jnp.maximum(m, higher(score(queries, old_rows(i, 1)))), most
+                )
+                last = jnp.where(ctx > whole * KEYS, 0.0, -1e30)
+                most = jnp.maximum(most, higher(last_old()) + last)
+                top[...] = jnp.where(own_lane, most * scale, 1e30)
+                total[...] = jnp.zeros_like(total)
+                mixed[...] = jnp.zeros_like(mixed)
+
+                @pl.loop(new_first, new_last + 1)
+                def _(i):
+                    mix(new_scores(i), new_turned[i])
+
+                @pl.loop(0, whole)
+                def _(i):
+                    mix(score(queries, old_rows(i, 1)), old_turned[i])
+
+                @pl.when(ctx > whole * KEYS)
+                def _():
+                    mix(last_old(), old_turned[whole])
+
+            out = mixed[...] / jnp.sum(total[...], axis=0, keepdims=True)
+            side = jnp.concatenate([out[:, h * TILE : (h + 1) * TILE] for h in range(3)], axis=0)
+            row = lax.broadcasted_iota(jnp.int32, side.shape, 1) + first
             mine = (row >= begin) & (row < end)
-            attn_ref[at, :] = jnp.where(mine, side, attn_ref[at, :].astype(F32)).astype(BF16)
+            attn_turned[t] = jnp.where(mine, side, attn_turned[t])
             return 0
 
         lax.fori_loop(begin // TILE, (end + TILE - 1) // TILE, tile, 0)
@@ -248,8 +310,13 @@
 
     kv_wide[pl.ds(tokens, 16), :] = jnp.zeros((16, 128), F32)
     kvx_ref[...] = jnp.zeros_like(kvx_ref)
-    attn_ref[...] = jnp.zeros_like(attn_ref)
+    attn_turned[...] = jnp.zeros_like(attn_turned)
     lax.fori_loop(0, 4, prompt, (0, 0))
+
+    @pl.loop(0, tokens // TILE)
+    def _(t):
+        attn_ref[pl.ds(pl.multiple_of(t * TILE, TILE), TILE), :] = attn_turned[t].T.astype(BF16)
+
     expert = lax.broadcasted_iota(jnp.int32, (32, 128), 0)
     gates = jnp.zeros((32, 128), F32)
     for k in range(8):
@@ -259,8 +326,7 @@
 
     x, z = group // 4, group % 4
 
-    @pl.loop(0, 18)
-    def _(i):
+    for i in range(18):
         asked, member = prompt_ref[i] // 4, prompt_ref[i] % 4
         first = ((asked // 4 - x + 4) % 4 * 4 + (asked % 4 - z + 4) % 4) * KV_ROWS
         for j in range(3):
@@ -283,9 +349,13 @@
         out_specs=(vmem(), vmem(), smem()),
         scratch_shapes=[
             pltpu.VMEM((tokens + 16, 128), F32),
-            pltpu.VMEM((3 * TILE, 1), F32),
-            pltpu.VMEM((3 * TILE, 1), F32),
-            pltpu.VMEM((3 * TILE, 128), F32),
+            pltpu.VMEM((cache.shape[1] // KEYS + 1, 64, KEYS), BF16),
+            pltpu.VMEM((tokens // KEYS, 64, KEYS), BF16),
+            pltpu.VMEM((tokens // TILE, 192, TILE), F32),
+            pltpu.VMEM((KEYS, 3 * TILE), F32),
+            pltpu.VMEM((1, 3 * TILE), F32),
+            pltpu.VMEM((8, 3 * TILE), F32),
+            pltpu.VMEM((64, 3 * TILE), F32),
         ],
         compiler_params=pltpu.CompilerParams(vmem_limit_bytes=VMEM_BYTES),
     )(q, kv, cache, routes_t, gates_t, span_t, ctx, req_prompt, cache_slot)

time: 193 us -> 231 us (1.20)
  Pallas kernels: 184 us -> 222 us
    pallas_call x1, Pallas kernels: 114 us -> 138 us  [finish(): pl.pallas_call(finish_kernel, name='finish', out_shape=(jax.ShapeDtypeStr...]
    pallas_call x1, Pallas kernels: 47.6 us -> 61.7 us  [attend(): pl.pallas_call(attend_kernel, name='attend', out_shape=(jax.ShapeDtypeStr...]
where the time goes in v2:
time: 231 us
  Pallas kernels  222 us (96%)
  local copies, waits for them, and re-layouts  7.62 us (3%)
    pallas_call x1, Pallas kernels, finish(): pl.pallas_call(finish_kernel, name='finish', out_shape=(jax.ShapeDtypeStr...  138 us
    pallas_call x1, Pallas kernels, attend(): pl.pallas_call(attend_kernel, name='attend', out_shape=(jax.ShapeDtypeStr...  61.7 us
    pallas_call x1, Pallas kernels, project_tokens(): pl.pallas_call(project_kernel, name='project_tokens', out_shape=(jax.Shap...  23 us
    unnamed x2, local copies, waits for them, and re-layouts  5.04 us

profile of v2, /device:TPU:0, one launch (start us, length us, event | category | flops | bytes accessed | tf_op | source)
XLA Modules:
  0.0 231.1 jit_solution(15609550781448995467)
XLA Ops:
  0.6 0.5 fusion.2.freq_ref
  1.2 1.3 broadcast_in_dim.7.gain_ref
  2.4 1.3 broadcast_in_dim.8.gain_ref
  3.7 23.0 %project_tokens.1 = (bf16[1024,384]{1,0:T(8,128)(2,1)}, bf16[1024,128]{1,0:T(8,128)(2,1)}) custom-call(bf16[128,1536]{1,0:T(8,128)(2,1)} %hidden_ref.3, f32[1,1536]{1,0:T(1,128)} %broadcast_in_dim.7.gain_ref, bf16[192,1536]{1,0:T(8,128)(2,1)} %bitcast.11, bf16[1536,128]{1,0:T(8,128)(2,1)} %bitcast.12, f32[1,128]{1,0:T(1,128)} %fusion.2.freq_ref, ...), custom_call_target="tpu_custom_call" | custom-call | tf_op jit(solution)/shard_map/project_tokens/pallas_call | solution.py:152
  26.8 61.7 %attend.1 = (bf16[1024,192]{1,0:T(8,128)(2,1)}, bf16[1152,128]{1,0:T(8,128)(2,1)}, s32[2,18]{1,0:T(2,128)}) custom-call(bf16[1024,384]{1,0:T(8,128)(2,1)} %get-tuple-element.9.q_ref, bf16[1024,128]{1,0:T(8,128)(2,1)} %get-tuple-element.10.kv_ref, bf16[4,2048,128]{2,1,0:T(8,128)(2,1)} %bitcast.10, s32[8,128]{1,0:T(8,128)} %bitcast.15, ...), custom_call_target="tpu_custom_call" | custom-call | tf_op jit(solution)/shard_map/attend/pallas_call | solution.py:340
  88.5 137.5 %finish.1 = (bf16[128,1536]{1,0:T(8,128)(2,1)}, bf16[18,512,128]{2,1,0:T(8,128)(2,1)}) custom-call(bf16[1024,192]{1,0:T(8,128)(2,1)} %get-tuple-element.11.attn_ref, bf16[192,1536]{1,0:T(8,128)(2,1)} %wout_ref.1, bf16[128,1536]{1,0:T(8,128)(2,1)} %hidden_ref.3, f32[1,1536]{1,0:T(1,128)} %broadcast_in_dim.8.gain_ref, ...), custom_call_target="tpu_custom_call" | custom-call | tf_op jit(solution)/shard_map/finish/pallas_call | solution.py:778
  226.0 1.8 copy.20
  227.8 3.3 %copy.21 = bf16[18,512,1,128]{3,1,2,0:T(8,128)(2,1)} copy(bf16[18,512,1,128]{3,1,2,0:T(8,128)(2,1)} %bitcast.9) | data formatting | bytes 4718592

commit v3 on v2

--- a/solution.py
+++ b/solution.py
@@ -2,6 +2,7 @@
 
 import jax
 import jax.numpy as jnp
+import numpy as np
 from jax import lax
 from jax.experimental import pallas as pl
 from jax.experimental.pallas import tpu as pltpu
@@ -62,7 +63,7 @@
     group = lax.axis_index("req")
     y, c, partner, up, down = head_neighbours()
     wait_all = greet([("head", partner), ("head", up), ("head", down)])
-    tok[0] = rms(hidden_ref[...].astype(F32), gain_ref[...]).astype(BF16)
+    tok[0] = rms(hidden_ref[...].astype(F32), gain_ref[...].reshape(1, -1)).astype(BF16)
     wait_all()
 
     def copy(i, src, dst, to):
@@ -73,16 +74,19 @@
 
     low, high = pl.ds(0, half), pl.ds(half, half)
     copies = [
-        copy(0, tok.at[0], tok.at[6], up),
-        copy(1, tok.at[0], tok.at[2], down),
+        copy(0, tok.at[0, low], tok.at[6, low], up),
+        copy(1, tok.at[0, high], tok.at[2, high], down),
         copy(2, tok.at[0], tok.at[1], partner),
         copy(3, tok.at[6, low], tok.at[4, low], up),
         copy(4, tok.at[6], tok.at[7], partner),
         copy(5, tok.at[2, high], tok.at[4, high], down),
         copy(6, tok.at[2], tok.at[3], partner),
-        copy(7, tok.at[4], tok.at[5], partner),
+        copy(7, tok.at[4, low], tok.at[5, low], partner),
+        copy(8, tok.at[0, high], tok.at[6, high], up),
+        copy(9, tok.at[0, low], tok.at[2, low], down),
+        copy(10, tok.at[4, high], tok.at[5, high], partner),
     ]
-    for i in (0, 1, 2):
+    for i in (0, 1, 8, 9, 2):
         copies[i].start()
 
     wq_wide[...] = jnp.zeros_like(wq_wide)
@@ -121,26 +125,30 @@
             q_ref[at, h * 128 : (h + 1) * 128] = turn(wide[:, h * 128 : (h + 1) * 128])
         kv_ref[at, :] = turn(jnp.dot(own, wkv_ref[...], preferred_element_type=F32))
 
-    project(0)
     copies[0].wait_recv()
     copies[3].start()
-    copies[4].start()
     copies[1].wait_recv()
     copies[5].start()
-    copies[6].start()
+    project(0)
     copies[2].wait_recv()
     project(1)
+    copies[8].wait_recv()
+    copies[4].start()
+    copies[9].wait_recv()
+    copies[6].start()
     project(6)
     project(2)
     copies[3].wait_recv()
+    copies[7].start()
     copies[5].wait_recv()
-    copies[7].start()
+    copies[10].start()
     copies[4].wait_recv()
     project(7)
     copies[6].wait_recv()
     project(3)
     project(4)
     copies[7].wait_recv()
+    copies[10].wait_recv()
     project(5)
     for one in copies:
         one.wait_send()
@@ -163,8 +171,8 @@
             pltpu.VMEM((384, width), BF16),
             pltpu.VMEM((tokens, 128), F32),
             pltpu.VMEM((tokens, 128), F32),
-            pltpu.SemaphoreType.DMA((8,)),
-            pltpu.SemaphoreType.DMA((8,)),
+            pltpu.SemaphoreType.DMA((11,)),
+            pltpu.SemaphoreType.DMA((11,)),
         ],
         compiler_params=pltpu.CompilerParams(
             collective_id=0, has_side_effects=True, vmem_limit_bytes=VMEM_BYTES
@@ -456,7 +464,7 @@
 def finish_kernel(
     attn_ref, wout_ref, hidden_ref, gain_ref, kvx_ref, place_ref, wgu_hbm, wd_hbm,
     out_ref, cache_hbm,
-    wgu, wd, part, pin, head_half, head_full, resid, kvall, rows_in, sums, red_half, red_full,
+    wgu, wd, part, pin, head_half, head_full, kept, resid, kvall, rows_in, sums, red_half, red_full,
     gates, ranks, picked, acts, outs, staged,
     wsem, csem, hssem, hrsem, kssem, krsem, assem, arsem, rssem, rrsem,
 ):
@@ -492,86 +500,112 @@
     row_steps = gather_steps(row_lines)
     kv_steps[0]()
 
-    def project(dy, dc, store, extra=()):
+    wide = width // 2
+
+    def project(dy, dc, piece, store):
         target = ((y + dy) % 4) * 2 + (c + dc) % 2
         own = attn_ref[pl.ds(pl.multiple_of(target * 128, 128), 128), :]
 
-        @pl.loop(0, width // 256)
+        @pl.loop(0, wide // 256)
         def _(n):
-            cols = pl.ds(pl.multiple_of(n * 256, 256), 256)
-            total = jnp.dot(own, wout_ref[:, cols], preferred_element_type=F32)
-            store(cols, total)
-
-    def into(index):
-        def store(cols, total):
-            part[index, :, cols] = total.astype(BF16)
-
-        return store
+            cols = pl.ds(pl.multiple_of(piece * wide + n * 256, 256), 256)
+            store(cols, jnp.dot(own, wout_ref[:, cols], preferred_element_type=F32))
 
     make = remote("head")
     low, high = pl.ds(0, 64), pl.ds(64, 64)
-    to_partner = {
-        dy: make(part.at[2 * dy + 1], pin.at[dy], hssem.at[dy], hrsem.at[dy], partner) for dy in range(4)
-    }
-    halves = [
-        make(part.at[4, low], head_half.at[0], hssem.at[4], hrsem.at[4], up),
-        make(part.at[4, high], head_half.at[1], hssem.at[5], hrsem.at[5], down),
+    pieces = [pl.ds(i * wide, wide) for i in range(2)]
+    to_partner = [
+        [
+            make(part.at[2 * dy + 1, :, p], pin.at[dy, :, p], hssem.at[8 * i + dy], hrsem.at[8 * i + dy], partner)
+            for i, p in enumerate(pieces)
+        ]
+        for dy in range(4)
     ]
-    fulls = [
-        make(part.at[2], head_full.at[0], hssem.at[6], hrsem.at[6], up),
-        make(part.at[6], head_full.at[1], hssem.at[7], hrsem.at[7], down),
-    ]
-    for dy in (2, 1, 3, 0):
-        project(dy, 1, into(2 * dy + 1))
-        to_partner[dy].start()
-
-    to_partner[2].wait_recv()
-
-    def store_two(cols, total):
-        part[4, :, cols] = (total + pin[2, :, cols].astype(F32)).astype(BF16)
-
-    project(2, 0, store_two)
-    for one in halves:
-        one.start()
+    halves, fulls = [], []
+    for i, p in enumerate(pieces):
+        at = 8 * i + 4
+        halves.append(
+            [
+                make(part.at[4, low, p], head_half.at[0, :, p], hssem.at[at], hrsem.at[at], up),
+                make(part.at[4, high, p], head_half.at[1, :, p], hssem.at[at + 1], hrsem.at[at + 1], down),
+            ]
+        )
+        fulls.append(
+            [
+                make(part.at[2, :, p], head_full.at[0, :, p], hssem.at[at + 2], hrsem.at[at + 2], up),
+                make(part.at[6, :, p], head_full.at[1, :, p], hssem.at[at + 3], hrsem.at[at + 3], down),
+            ]
+        )
+
+    def give(dy, piece):
+        def store(cols, total):
+            part[2 * dy + 1, :, cols] = total.astype(BF16)
+
+        project(dy, 1, piece, store)
+        to_partner[dy][piece].start()
+
+    for i in range(2):
+        give(2, i)
+    for i in range(2):
+        to_partner[2][i].wait_recv()
+
+        def store_far(cols, total):
+            part[4, :, cols] = (total + pin[2, :, cols].astype(F32)).astype(BF16)
+
+        project(2, 0, i, store_far)
+        halves[i][0].start()
+        halves[i][1].start()
+    for dy in (1, 3, 0):
+        for i in range(2):
+            give(dy, i)
+    for k, dy in enumerate((1, 3, 0)):
+        for i in range(2):
+
+            def store_own(cols, total, k=k, dy=dy):
+                kept[k, :, cols] = total + hidden_ref[:, cols].astype(F32) if dy == 0 else total
+
+            project(dy, 0, i, store_own)
     kv_steps[1]()
-    to_partner[1].wait_recv()
-    halves[0].wait_recv()
-
-    def store_one(cols, total):
-        total = total + pin[1, :, cols].astype(F32)
-        part[2, low, cols] = (total[:64] + head_half[0, :, cols].astype(F32)).astype(BF16)
-        part[2, high, cols] = total[64:].astype(BF16)
-
-    project(1, 0, store_one)
-    fulls[0].start()
-    to_partner[3].wait_recv()
-    halves[1].wait_recv()
-
-    def store_three(cols, total):
-        total = total + pin[3, :, cols].astype(F32)
-        part[6, low, cols] = total[:64].astype(BF16)
-        part[6, high, cols] = (total[64:] + head_half[1, :, cols].astype(F32)).astype(BF16)
-
-    project(3, 0, store_three)
-    fulls[1].start()
+
+    def pass_on(k, dy, index, side, piece):
+        to_partner[dy][piece].wait_recv()
+        halves[piece][side].wait_recv()
+        reached = (0, 4) if side == 0 else (4, 8)
+        for lo, hi, with_half in ((*reached, True), ((4, 8) if side == 0 else (0, 4)) + (False,)):
+
+            @pl.loop(0, 4)
+            def _(n, lo=lo, with_half=with_half):
+                at = pl.ds(pl.multiple_of(lo * 16 + n * 16, 16), 16)
+                cols = pieces[piece]
+                total = kept[k, at, cols] + pin[dy, at, cols].astype(F32)
+                if with_half:
+                    total = total + head_half[side, pl.ds(pl.multiple_of(n * 16, 16), 16), cols].astype(F32)
+                part[index, at, cols] = total.astype(BF16)
+
+        fulls[piece][side].start()
+
+    for i in range(2):
+        pass_on(0, 1, 2, 0, i)
+        pass_on(1, 3, 6, 1, i)
     kv_steps[2]()
     kv_steps[3]()
     kv_steps[4]()
-    to_partner[0].wait_recv()
-    fulls[0].wait_recv()
-    fulls[1].wait_recv()
-
-    def store_own(cols, total):
-        total = total + pin[0, :, cols].astype(F32) + hidden_ref[:, cols].astype(F32)
-        total = total + head_full[0, :, cols].astype(F32) + head_full[1, :, cols].astype(F32)
-        resid[:, cols] = total
-
-    project(0, 0, store_own)
-
-    @pl.loop(0, 8)
+    for i in range(2):
+        to_partner[0][i].wait_recv()
+        fulls[i][0].wait_recv()
+        fulls[i][1].wait_recv()
+
+        @pl.loop(0, 8)
+        def _(n, i=i):
+            at = pl.ds(pl.multiple_of(n * 16, 16), 16)
+            cols = pieces[i]
+            total = kept[2, at, cols] + pin[0, at, cols].astype(F32)
+            resid[at, cols] = total + head_full[0, at, cols].astype(F32) + head_full[1, at, cols].astype(F32)
+
+    @pl.loop(0, 8, unroll=4)
     def _(i):
         at = pl.ds(pl.multiple_of(i * 16, 16), 16)
-        rows_in[0, at, :] = rms(resid[at, :], gain_ref[...]).astype(BF16)
+        rows_in[0, at, :] = rms(resid[at, :], gain_ref[...].reshape(1, -1)).astype(BF16)
 
     row_steps[0]()
     kv_steps[5]()
@@ -761,10 +795,9 @@
             total = total + red_full[n, 0, at, :].astype(F32) + red_full[n, 1, at, :].astype(F32)
             out_ref[to, :] = total.astype(BF16)
 
-    for dy in range(4):
-        to_partner[dy].wait_send()
-    for one in halves + fulls:
-        one.wait_send()
+    for some in to_partner + halves + fulls:
+        for one in some:
+            one.wait_send()
     kv_steps[9]()
     row_steps[9]()
     for line in range(5):
@@ -791,6 +824,7 @@
             pltpu.VMEM((4, rows, width), BF16),
             pltpu.VMEM((2, rows // 2, width), BF16),
             pltpu.VMEM((2, rows, width), BF16),
+            pltpu.VMEM((3, rows, width), F32),
             pltpu.VMEM((rows, width), F32),
             pltpu.VMEM((16 * KV_ROWS + 512, 128), BF16),
             pltpu.VMEM((16, rows, width), BF16),
@@ -805,8 +839,8 @@
             pltpu.VMEM((18, 512, 128), BF16),
             pltpu.SemaphoreType.DMA((3,)),
             pltpu.SemaphoreType.DMA((1,)),
-            pltpu.SemaphoreType.DMA((8,)),
-            pltpu.SemaphoreType.DMA((8,)),
+            pltpu.SemaphoreType.DMA((16,)),
+            pltpu.SemaphoreType.DMA((16,)),
             pltpu.SemaphoreType.DMA((40,)),
             pltpu.SemaphoreType.DMA((40,)),
             pltpu.SemaphoreType.DMA((40,)),
@@ -827,17 +861,16 @@
     width = hidden_in.shape[1]
     prompts_dev = cache_kv.shape[0]
     span_t = span_len.T
-    lane = jnp.arange(128)
-    freq = (ROPE_BASE ** (-2.0 * (lane % 32).astype(F32) / 64.0))[None, :]
+    freq = (ROPE_BASE ** (-2.0 * (np.arange(128) % 32) / 64.0)).astype(np.float32)[None, :]
     q, kv = project_tokens(
-        hidden_in, attn_gain[None, :], w_query.T, keyvalue_weight.reshape(width, 128), freq, span_t, ctx_len
+        hidden_in, attn_gain, w_query.T, keyvalue_weight.reshape(width, 128), freq, span_t, ctx_len
     )
     attn, kvx, place_rows = attend(
         q, kv, cache_kv.reshape(prompts_dev, -1, 128), routes.T, gate_weights.T, span_t, ctx_len,
         req_prompt, cache_slot,
     )
     layer_out, cache = finish(
-        attn, w_out, hidden_in, ffn_gain[None, :], kvx, place_rows, w_gate_up, w_down
+        attn, w_out, hidden_in, ffn_gain, kvx, place_rows, w_gate_up, w_down
     )
     return (layer_out, cache.reshape(18, 512, 1, 128))
 

time: 231 us -> 231 us (level)
  Pallas kernels: 222 us -> 225 us
  local copies, waits for them, and re-layouts: 7.62 us -> 5.04 us
    pallas_call x1, Pallas kernels: 61.7 us -> 69.9 us  [attend(): pl.pallas_call(attend_kernel, name='attend', out_shape=(jax.ShapeDtypeStr...]
    pallas_call x1, Pallas kernels: 138 us -> 132 us  [finish(): pl.pallas_call(finish_kernel, name='finish', out_shape=(jax.ShapeDtypeStr...]
    broadcast_in_dim x2 -> x0, local copies, waits for them, and re-layouts: 2.58 us -> none  [the longest x1 1.29 us: body(): attn_gain[None, :]]
where the time goes in v3:
time: 231 us; the launch traced here: 230 us
  Pallas kernels  225 us (97%)
  local copies, waits for them, and re-layouts  5.04 us (2%)
    pallas_call x1, Pallas kernels, finish(): pl.pallas_call(finish_kernel, name='finish', out_shape=(jax.ShapeDtypeStr...  132 us
    pallas_call x1, Pallas kernels, attend(): pl.pallas_call(attend_kernel, name='attend', out_shape=(jax.ShapeDtypeStr...  69.9 us
    pallas_call x1, Pallas kernels, project_tokens(): pl.pallas_call(project_kernel, name='project_tokens', out_shape=(jax.Shap...  22.3 us
    unnamed x2, local copies, waits for them, and re-layouts  5.04 us

profile of v3, /device:TPU:0, one launch (start us, length us, event | category | flops | bytes accessed | tf_op | source)
XLA Modules:
  0.0 230.3 jit_solution(5540969847227464330)
XLA Ops:
  0.6 22.3 %project_tokens.1 = (bf16[1024,384]{1,0:T(8,128)(2,1)}, bf16[1024,128]{1,0:T(8,128)(2,1)}) custom-call(bf16[128,1536]{1,0:T(8,128)(2,1)} %hidden_ref.3, f32[1536]{0:T(1024)} %gain_ref.2, bf16[192,1536]{1,0:T(8,128)(2,1)} %bitcast.11, bf16[1536,128]{1,0:T(8,128)(2,1)} %bitcast.12, f32[1,128]{1,0:T(1,128)} %constant.2.clone.freq_ref, s32[4,16]{1,0:T(4,128)} %bitcast.13, ...), custom_call_target="tpu_custom_call" | custom-call | tf_op jit(solution)/shard_map/project_tokens/pallas_call | solution.py:160
  22.9 69.9 %attend.1 = (bf16[1024,192]{1,0:T(8,128)(2,1)}, bf16[1152,128]{1,0:T(8,128)(2,1)}, s32[2,18]{1,0:T(2,128)}) custom-call(bf16[1024,384]{1,0:T(8,128)(2,1)} %get-tuple-element.9.q_ref, bf16[1024,128]{1,0:T(8,128)(2,1)} %get-tuple-element.10.kv_ref, bf16[4,2048,128]{2,1,0:T(8,128)(2,1)} %bitcast.10, s32[8,128]{1,0:T(8,128)} %bitcast.15, ...), custom_call_target="tpu_custom_call" | custom-call | tf_op jit(solution)/shard_map/attend/pallas_call | solution.py:348
  92.8 132.5 %finish.1 = (bf16[128,1536]{1,0:T(8,128)(2,1)}, bf16[18,512,128]{2,1,0:T(8,128)(2,1)}) custom-call(bf16[1024,192]{1,0:T(8,128)(2,1)} %get-tuple-element.11.attn_ref, bf16[192,1536]{1,0:T(8,128)(2,1)} %wout_ref.1, bf16[128,1536]{1,0:T(8,128)(2,1)} %hidden_ref.3, f32[1536]{0:T(1024)} %gain_ref.3, bf16[1152,128]{1,0:T(8,128)(2,1)} %get-tuple-element.12.kvx_ref, ...), custom_call_target="tpu_custom_call" | custom-call | tf_op jit(solution)/shard_map/finish/pallas_call | solution.py:811
  225.3 1.8 copy.21
  227.1 3.3 %copy.22 = bf16[18,512,1,128]{3,1,2,0:T(8,128)(2,1)} copy(bf16[18,512,1,128]{3,1,2,0:T(8,128)(2,1)} %bitcast.9) | data formatting | bytes 4718592

commit v4 on v3

--- a/solution.py
+++ b/solution.py
@@ -371,7 +371,8 @@
 
 GROUPS = (
     ((0, 0), (0, 1), (0, 3), (1, 0), (3, 0)),
-    ((0, 2), (2, 0), (1, 1), (1, 3), (3, 1), (3, 3)),
+    ((1, 1), (1, 3), (3, 1), (3, 3)),
+    ((0, 2), (2, 0)),
     ((2, 2), (2, 1), (2, 3), (1, 2), (3, 2)),
 )
 
@@ -500,130 +501,117 @@
     row_steps = gather_steps(row_lines)
     kv_steps[0]()
 
-    wide = width // 2
-
-    def project(dy, dc, piece, store):
+    def project(dy, dc, store):
         target = ((y + dy) % 4) * 2 + (c + dc) % 2
         own = attn_ref[pl.ds(pl.multiple_of(target * 128, 128), 128), :]
 
-        @pl.loop(0, wide // 256)
+        @pl.loop(0, width // 256)
         def _(n):
-            cols = pl.ds(pl.multiple_of(piece * wide + n * 256, 256), 256)
+            cols = pl.ds(pl.multiple_of(n * 256, 256), 256)
             store(cols, jnp.dot(own, wout_ref[:, cols], preferred_element_type=F32))
 
     make = remote("head")
     low, high = pl.ds(0, 64), pl.ds(64, 64)
-    pieces = [pl.ds(i * wide, wide) for i in range(2)]
     to_partner = [
-        [
-            make(part.at[2 * dy + 1, :, p], pin.at[dy, :, p], hssem.at[8 * i + dy], hrsem.at[8 * i + dy], partner)
-            for i, p in enumerate(pieces)
-        ]
-        for dy in range(4)
+        make(part.at[2 * dy + 1], pin.at[dy], hssem.at[dy], hrsem.at[dy], partner) for dy in range(4)
     ]
-    halves, fulls = [], []
-    for i, p in enumerate(pieces):
-        at = 8 * i + 4
-        halves.append(
-            [
-                make(part.at[4, low, p], head_half.at[0, :, p], hssem.at[at], hrsem.at[at], up),
-                make(part.at[4, high, p], head_half.at[1, :, p], hssem.at[at + 1], hrsem.at[at + 1], down),
-            ]
-        )
-        fulls.append(
-            [
-                make(part.at[2, :, p], head_full.at[0, :, p], hssem.at[at + 2], hrsem.at[at + 2], up),
-                make(part.at[6, :, p], head_full.at[1, :, p], hssem.at[at + 3], hrsem.at[at + 3], down),
-            ]
-        )
-
-    def give(dy, piece):
+
+    def ring_copy(i, src, dst, to):
+        return make(src, dst, hssem.at[4 + i], hrsem.at[4 + i], to)
+
+    far = (
+        ring_copy(0, part.at[4, low], head_half.at[0], up),
+        ring_copy(1, part.at[4, high], head_half.at[1], down),
+    )
+    free = (
+        ring_copy(2, part.at[2, high], head_full.at[0, high], up),
+        ring_copy(3, part.at[6, low], head_full.at[1, low], down),
+    )
+    bound = (
+        ring_copy(4, part.at[2, low], head_full.at[0, low], up),
+        ring_copy(5, part.at[6, high], head_full.at[1, high], down),
+    )
+
+    def give(dy):
         def store(cols, total):
             part[2 * dy + 1, :, cols] = total.astype(BF16)
 
-        project(dy, 1, piece, store)
-        to_partner[dy][piece].start()
-
-    for i in range(2):
-        give(2, i)
-    for i in range(2):
-        to_partner[2][i].wait_recv()
-
-        def store_far(cols, total):
-            part[4, :, cols] = (total + pin[2, :, cols].astype(F32)).astype(BF16)
-
-        project(2, 0, i, store_far)
-        halves[i][0].start()
-        halves[i][1].start()
-    for dy in (1, 3, 0):
-        for i in range(2):
-            give(dy, i)
-    for k, dy in enumerate((1, 3, 0)):
-        for i in range(2):
-
-            def store_own(cols, total, k=k, dy=dy):
-                kept[k, :, cols] = total + hidden_ref[:, cols].astype(F32) if dy == 0 else total
-
-            project(dy, 0, i, store_own)
+        project(dy, 1, store)
+        to_partner[dy].start()
+
+    def keep(k, dy):
+        def store(cols, total):
+            kept[k, :, cols] = total + hidden_ref[:, cols].astype(F32) if dy == 0 else total
+
+        project(dy, 0, store)
+
+    def sum_rows(k, dy, index, first, half=None):
+        @pl.loop(0, 4)
+        def _(n):
+            at = pl.ds(pl.multiple_of(first + n * 16, 16), 16)
+            total = kept[k, at, :] + pin[dy, at, :].astype(F32)
+            if half is not None:
+                total = total + head_half[half, pl.ds(pl.multiple_of(n * 16, 16), 16), :].astype(F32)
+            part[index, at, :] = total.astype(BF16)
+
+    give(2)
+    give(1)
+    give(3)
+    to_partner[2].wait_recv()
+
+    def store_far(cols, total):
+        part[4, :, cols] = (total + pin[2, :, cols].astype(F32)).astype(BF16)
+
+    project(2, 0, store_far)
+    far[0].start()
+    far[1].start()
+    keep(0, 1)
+    to_partner[1].wait_recv()
+    sum_rows(0, 1, 2, 64)
+    free[0].start()
+    keep(1, 3)
+    to_partner[3].wait_recv()
+    sum_rows(1, 3, 6, 0)
+    free[1].start()
+    give(0)
+    keep(2, 0)
     kv_steps[1]()
-
-    def pass_on(k, dy, index, side, piece):
-        to_partner[dy][piece].wait_recv()
-        halves[piece][side].wait_recv()
-        reached = (0, 4) if side == 0 else (4, 8)
-        for lo, hi, with_half in ((*reached, True), ((4, 8) if side == 0 else (0, 4)) + (False,)):
-
-            @pl.loop(0, 4)
-            def _(n, lo=lo, with_half=with_half):
-                at = pl.ds(pl.multiple_of(lo * 16 + n * 16, 16), 16)
-                cols = pieces[piece]
-                total = kept[k, at, cols] + pin[dy, at, cols].astype(F32)
-                if with_half:
-                    total = total + head_half[side, pl.ds(pl.multiple_of(n * 16, 16), 16), cols].astype(F32)
-                part[index, at, cols] = total.astype(BF16)
-
-        fulls[piece][side].start()
-
-    for i in range(2):
-        pass_on(0, 1, 2, 0, i)
-        pass_on(1, 3, 6, 1, i)
+    far[0].wait_recv()
+    sum_rows(0, 1, 2, 0, 0)
+    bound[0].start()
+    far[1].wait_recv()
+    sum_rows(1, 3, 6, 64, 1)
+    bound[1].start()
     kv_steps[2]()
     kv_steps[3]()
     kv_steps[4]()
-    for i in range(2):
-        to_partner[0][i].wait_recv()
-        fulls[i][0].wait_recv()
-        fulls[i][1].wait_recv()
-
-        @pl.loop(0, 8)
-        def _(n, i=i):
-            at = pl.ds(pl.multiple_of(n * 16, 16), 16)
-            cols = pieces[i]
-            total = kept[2, at, cols] + pin[0, at, cols].astype(F32)
-            resid[at, cols] = total + head_full[0, at, cols].astype(F32) + head_full[1, at, cols].astype(F32)
-
-    @pl.loop(0, 8, unroll=4)
-    def _(i):
-        at = pl.ds(pl.multiple_of(i * 16, 16), 16)
-        rows_in[0, at, :] = rms(resid[at, :], gain_ref[...].reshape(1, -1)).astype(BF16)
+    to_partner[0].wait_recv()
+    for one in free + bound:
+        one.wait_recv()
+
+    @pl.loop(0, 8, unroll=2)
+    def _(n):
+        at = pl.ds(pl.multiple_of(n * 16, 16), 16)
+        total = kept[2, at, :] + pin[0, at, :].astype(F32)
+        total = total + head_full[0, at, :].astype(F32) + head_full[1, at, :].astype(F32)
+        resid[at, :] = total
+        rows_in[0, at, :] = rms(total, gain_ref[...].reshape(1, -1)).astype(BF16)
 
     row_steps[0]()
     kv_steps[5]()
     kv_steps[6]()
-    kv_steps[7]()
-    kv_steps[8]()
     expert = lax.broadcasted_iota(jnp.int32, (32, 128), 0)
-
-    @pl.loop(0, 16)
-    def _(slot):
-        table = kvall[pl.ds(pl.multiple_of(slot * KV_ROWS + GATE_ROW, 16), 32), :].astype(F32)
-        for j in range(2):
-            mine = jnp.sum(jnp.where(expert == r * 2 + j, table, 0.0), axis=0, keepdims=True)
-            gates[pl.ds(slot * 2 + j, 1), :] = mine
-
     before = lax.broadcasted_iota(jnp.int32, (128, 128), 0) < lax.broadcasted_iota(jnp.int32, (128, 128), 1)
-    hits = jnp.where(gates[...] > 0.0, 1.0, 0.0).astype(BF16)
-    ranks[...] = jnp.dot(hits, jnp.where(before, 1.0, 0.0).astype(BF16), preferred_element_type=F32)
+    order = jnp.where(before, 1.0, 0.0).astype(BF16)
+
+    def read_gates(slots):
+        for slot in slots:
+            table = kvall[slot * KV_ROWS + GATE_ROW : slot * KV_ROWS + GATE_ROW + 32, :].astype(F32)
+            for j in range(2):
+                mine = jnp.sum(jnp.where(expert == r * 2 + j, table, 0.0), axis=0, keepdims=True)
+                gates[slot * 2 + j : slot * 2 + j + 1, :] = mine
+        hits = jnp.where(gates[...] > 0.0, 1.0, 0.0).astype(BF16)
+        ranks[...] = jnp.dot(hits, order, preferred_element_type=F32)
 
     def chosen(slot, weighted):
         place = lax.broadcasted_iota(jnp.int32, (CAP, 128), 0).astype(F32)
@@ -641,7 +629,7 @@
             slot = a * 4 + b
             select = chosen(slot, False)
 
-            @pl.loop(0, width // 512)
+            @pl.loop(0, width // 512, unroll=width // 512)
             def _(n, k=k, slot=slot, select=select):
                 cols = pl.ds(pl.multiple_of(n * 512, 512), 512)
                 got = jnp.dot(select, rows_in[slot, :, cols], preferred_element_type=F32).astype(BF16)
@@ -659,7 +647,7 @@
                 lift = jnp.dot(own, wgu[e, :, later], preferred_element_type=F32)
                 acts[pl.ds(0, count), cols] = (gate / (1.0 + jnp.exp(-gate)) * lift).astype(BF16)
 
-            @pl.loop(0, width // 256)
+            @pl.loop(0, width // 256, unroll=2)
             def _(n):
                 cols = pl.ds(pl.multiple_of(n * 256, 256), 256)
                 outs[e, pl.ds(0, count), cols] = jnp.dot(
@@ -670,7 +658,7 @@
             slot = a * 4 + b
             spread = chosen(slot, True)
 
-            @pl.loop(0, width // 512)
+            @pl.loop(0, width // 512, unroll=width // 512)
             def _(n, k=k, slot=slot, spread=spread):
                 cols = pl.ds(pl.multiple_of(n * 512, 512), 512)
                 given = jnp.concatenate(
@@ -679,6 +667,19 @@
                 sums[slot, :, cols] = lax.dot_general(
                     spread, given, (((0,), (0,)), ((), ())), preferred_element_type=F32
                 ).astype(BF16)
+
+    store = pltpu.make_async_copy(staged, cache_hbm, csem.at[0])
+
+    def fill_cache():
+        @pl.loop(0, 18)
+        def _(s):
+            start, length = place_ref[0, s], place_ref[1, s]
+            for i in range(4):
+                rows = kvall[pl.ds(start * 16 + i * 128, 128), :].astype(F32)
+                at = lax.broadcasted_iota(jnp.int32, (128, 128), 0) + i * 128
+                staged[s, pl.ds(i * 128, 128), :] = jnp.where(at < length, rows, 0.0).astype(BF16)
+
+        store.start()
 
     def add(dst, row, src, count):
         @pl.loop(0, count // 16)
@@ -697,30 +698,38 @@
         def piece(k, row, count):
             return sums.at[at(k), pl.ds(base + row, count), :]
 
-        s = [rssem.at[4 * n + i] for i in range(4)]
-        g = [rrsem.at[4 * n + i] for i in range(4)]
+        def copy(i, src, dst, to):
+            return send(src, dst, rssem.at[6 * n + i], rrsem.at[6 * n + i], to)
+
+        first, second = pl.ds(0, 32), pl.ds(32, 32)
         copies = [
-            send(piece(2, 0, 32), red_half.at[n, 0], s[0], g[0], plus),
-            send(piece(2, 32, 32), red_half.at[n, 1], s[1], g[1], minus),
-            send(piece(1, 0, 64), red_full.at[n, 0], s[2], g[2], plus),
-            send(piece(3, 0, 64), red_full.at[n, 1], s[3], g[3], minus),
+            copy(0, piece(2, 0, 32), red_half.at[n, 0], plus),
+            copy(1, piece(2, 32, 32), red_half.at[n, 1], minus),
+            copy(2, piece(1, 32, 32), red_full.at[n, 0, second], plus),
+            copy(3, piece(3, 0, 32), red_full.at[n, 1, first], minus),
+            copy(4, piece(1, 0, 32), red_full.at[n, 0, first], plus),
+            copy(5, piece(3, 32, 32), red_full.at[n, 1, second], minus),
         ]
 
-        def out():
+        def far():
             copies[0].start()
             copies[1].start()
+
+        def near():
+            copies[2].start()
+            copies[3].start()
 
         def middle():
             copies[0].wait_recv()
             add(at(1), base, [red_half.at[n, 0]], 32)
-            copies[2].start()
+            copies[4].start()
             copies[1].wait_recv()
             add(at(3), base + 32, [red_half.at[n, 1]], 32)
-            copies[3].start()
+            copies[5].start()
 
         def last():
-            copies[2].wait_recv()
-            copies[3].wait_recv()
+            for one in copies[2:]:
+                one.wait_recv()
 
         def fold():
             last()
@@ -730,7 +739,7 @@
             for one in copies:
                 one.wait_send()
 
-        return out, middle, fold, last, drain
+        return {"far": far, "near": near, "middle": middle, "fold": fold, "last": last, "drain": drain}
 
     back = []
     for which in (0, 1):
@@ -747,45 +756,40 @@
         for these in back:
             these[line][step]()
 
+    near = [a * 4 + b for a, b in GROUPS[0]]
+    gates[...] = jnp.zeros_like(gates)
+    read_gates(near)
+    for one in loads[:2]:
+        one.wait()
     row_steps[1]()
     row_steps[2]()
-    for one in loads[:2]:
-        one.wait()
     experts(GROUPS[0])
+    kv_steps[7]()
+    kv_steps[8]()
     row_steps[3]()
     row_steps[4]()
-
-    @pl.loop(0, 18)
-    def _(s):
-        start, length = place_ref[0, s], place_ref[1, s]
-        for i in range(4):
-            rows = kvall[pl.ds(start * 16 + i * 128, 128), :].astype(F32)
-            at = lax.broadcasted_iota(jnp.int32, (128, 128), 0) + i * 128
-            staged[s, pl.ds(i * 128, 128), :] = jnp.where(at < length, rows, 0.0).astype(BF16)
-
-    store = pltpu.make_async_copy(staged, cache_hbm, csem.at[0])
-    store.start()
+    read_gates([slot for slot in range(16) if slot not in near])
+
+    experts(GROUPS[1])
     row_steps[5]()
-    experts(GROUPS[1])
-    go(0, 0)
     row_steps[6]()
+    experts(GROUPS[2])
     row_steps[7]()
-    go(0, 1)
+    go(0, "far")
+    go(0, "near")
     row_steps[8]()
-    experts(GROUPS[2])
-    go(2, 0)
-    go(1, 0)
-    go(3, 0)
-    go(0, 2)
-    go(2, 1)
-    go(1, 1)
-    go(3, 1)
-    go(2, 2)
-    go(4, 0)
-    go(1, 2)
-    go(3, 2)
-    go(4, 1)
-    go(4, 3)
+    experts(GROUPS[3])
+    go(0, "middle")
+    for line, step in (
+        (2, "far"), (2, "near"), (1, "far"), (1, "near"), (3, "far"), (3, "near"), (0, "fold"), (2, "middle"),
+        (1, "middle"), (3, "middle"),
+    ):
+        go(line, step)
+    fill_cache()
+    for line, step in (
+        (2, "fold"), (4, "far"), (1, "fold"), (3, "fold"), (4, "near"), (4, "middle"), (4, "last"),
+    ):
+        go(line, step)
     for which, n in ((0, 4), (1, 9)):
         @pl.loop(0, 4)
         def _(i, which=which, n=n):
@@ -795,13 +799,12 @@
             total = total + red_full[n, 0, at, :].astype(F32) + red_full[n, 1, at, :].astype(F32)
             out_ref[to, :] = total.astype(BF16)
 
-    for some in to_partner + halves + fulls:
-        for one in some:
-            one.wait_send()
+    for one in (*to_partner, *far, *free, *bound):
+        one.wait_send()
     kv_steps[9]()
     row_steps[9]()
     for line in range(5):
-        go(line, 4)
+        go(line, "drain")
     store.wait()
 
 
@@ -839,14 +842,14 @@
             pltpu.VMEM((18, 512, 128), BF16),
             pltpu.SemaphoreType.DMA((3,)),
             pltpu.SemaphoreType.DMA((1,)),
-            pltpu.SemaphoreType.DMA((16,)),
-            pltpu.SemaphoreType.DMA((16,)),
+            pltpu.SemaphoreType.DMA((10,)),
+            pltpu.SemaphoreType.DMA((10,)),
             pltpu.SemaphoreType.DMA((40,)),
             pltpu.SemaphoreType.DMA((40,)),
             pltpu.SemaphoreType.DMA((40,)),
             pltpu.SemaphoreType.DMA((40,)),
-            pltpu.SemaphoreType.DMA((40,)),
-            pltpu.SemaphoreType.DMA((40,)),
+            pltpu.SemaphoreType.DMA((60,)),
+            pltpu.SemaphoreType.DMA((60,)),
         ],
         compiler_params=pltpu.CompilerParams(
             collective_id=1, has_side_effects=True, vmem_limit_bytes=VMEM_BYTES

time: 231 us -> 232 us (level)
    pallas_call x1, Pallas kernels: 69.9 us -> 86.5 us  [attend(): pl.pallas_call(attend_kernel, name='attend', out_shape=(jax.ShapeDtypeStr...]
    pallas_call x1, Pallas kernels: 132 us -> 117 us  [finish(): pl.pallas_call(finish_kernel, name='finish', out_shape=(jax.ShapeDtypeStr...]
where the time goes in v4:
time: 232 us
  Pallas kernels  226 us (97%)
  local copies, waits for them, and re-layouts  5.04 us (2%)
    pallas_call x1, Pallas kernels, finish(): pl.pallas_call(finish_kernel, name='finish', out_shape=(jax.ShapeDtypeStr...  117 us
    pallas_call x1, Pallas kernels, attend(): pl.pallas_call(attend_kernel, name='attend', out_shape=(jax.ShapeDtypeStr...  86.5 us
    pallas_call x1, Pallas kernels, project_tokens(): pl.pallas_call(project_kernel, name='project_tokens', out_shape=(jax.Shap...  22.3 us
    unnamed x2, local copies, waits for them, and re-layouts  5.04 us

profile of v4, /device:TPU:0, one launch (start us, length us, event | category | flops | bytes accessed | tf_op | source)
XLA Modules:
  0.0 231.9 jit_solution(13859114442591309704)
XLA Ops:
  0.6 22.3 %project_tokens.1 = (bf16[1024,384]{1,0:T(8,128)(2,1)}, bf16[1024,128]{1,0:T(8,128)(2,1)}) custom-call(bf16[128,1536]{1,0:T(8,128)(2,1)} %hidden_ref.3, f32[1536]{0:T(1024)} %gain_ref.2, bf16[192,1536]{1,0:T(8,128)(2,1)} %bitcast.11, bf16[1536,128]{1,0:T(8,128)(2,1)} %bitcast.12, f32[1,128]{1,0:T(1,128)} %constant.2.clone.freq_ref, s32[4,16]{1,0:T(4,128)} %bitcast.13, ...), custom_call_target="tpu_custom_call" | custom-call | tf_op jit(solution)/shard_map/project_tokens/pallas_call | solution.py:160
  22.9 86.5 %attend.1 = (bf16[1024,192]{1,0:T(8,128)(2,1)}, bf16[1152,128]{1,0:T(8,128)(2,1)}, s32[2,18]{1,0:T(2,128)}) custom-call(bf16[1024,384]{1,0:T(8,128)(2,1)} %get-tuple-element.9.q_ref, bf16[1024,128]{1,0:T(8,128)(2,1)} %get-tuple-element.10.kv_ref, bf16[4,2048,128]{2,1,0:T(8,128)(2,1)} %bitcast.10, s32[8,128]{1,0:T(8,128)} %bitcast.15, ...), custom_call_target="tpu_custom_call" | custom-call | tf_op jit(solution)/shard_map/attend/pallas_call | solution.py:348
  109.4 117.4 %finish.1 = (bf16[128,1536]{1,0:T(8,128)(2,1)}, bf16[18,512,128]{2,1,0:T(8,128)(2,1)}) custom-call(bf16[1024,192]{1,0:T(8,128)(2,1)} %get-tuple-element.11.attn_ref, bf16[192,1536]{1,0:T(8,128)(2,1)} %wout_ref.1, bf16[128,1536]{1,0:T(8,128)(2,1)} %hidden_ref.3, f32[1536]{0:T(1024)} %gain_ref.3, bf16[1152,128]{1,0:T(8,128)(2,1)} %get-tuple-element.12.kvx_ref, ...), custom_call_target="tpu_custom_call" | custom-call | tf_op jit(solution)/shard_map/finish/pallas_call | solution.py:814
  226.8 1.8 copy.21
  228.6 3.3 %copy.22 = bf16[18,512,1,128]{3,1,2,0:T(8,128)(2,1)} copy(bf16[18,512,1,128]{3,1,2,0:T(8,128)(2,1)} %bitcast.9) | data formatting | bytes 4718592

commit v5 on v4

--- a/solution.py
+++ b/solution.py
@@ -188,7 +188,7 @@
 def attend_kernel(
     q_ref, kv_ref, cache_ref, routes_ref, gates_ref, span_ref, ctx_ref, prompt_ref, place_ref,
     attn_ref, kvx_ref, place_rows_ref,
-    kv_wide, old_turned, new_turned, attn_turned, near, top, total, mixed,
+    kv_wide, old_turned, new_turned, attn_turned, near, top, total, mixed, largest,
 ):
     group = lax.axis_index("req")
     tokens = q_ref.shape[0]
@@ -210,20 +210,19 @@
     def _(i):
         new_turned[i] = new_rows(i).T[64:, :]
 
-    def prompt(j, carry):
+    def prompt(j, carry, exact):
         begin, packed = carry
         length = span_ref[j, group]
         end = begin + length
         ctx = ctx_ref[group * 4 + j]
-        long = ctx // (LONG * KEYS)
-        whole = ctx // KEYS
+        last = (ctx - 1) // KEYS
+        long = last // LONG
         new_first = begin // KEYS
-        most_chunks = cache_ref.shape[1] // KEYS
 
         def old_rows(i, count):
             return cache_ref[j, pl.ds(pl.multiple_of(i * KEYS, KEYS), count * KEYS), :]
 
-        @pl.loop(0, (ctx + KEYS - 1) // KEYS)
+        @pl.loop(0, last + 1)
         def _(i):
             old_turned[i] = old_rows(i, 1).T[64:, :]
 
@@ -231,8 +230,6 @@
             first = pl.multiple_of(t * TILE, TILE)
             at = pl.ds(first, TILE)
             queries = jnp.concatenate([q_ref[at, h * 128 : (h + 1) * 128] for h in range(3)], axis=0)
-            total[...] = jnp.zeros_like(total)
-            mixed[...] = jnp.zeros_like(mixed)
             lane_row = lax.broadcasted_iota(jnp.int32, (1, 3 * TILE), 1) % TILE + first
             own_lane = (lane_row >= begin) & (lane_row < end)
             new_last = (first + TILE - 1) // KEYS
@@ -244,61 +241,51 @@
                 bias = jnp.where((key >= begin) & (key <= row), 0.0, -1e30)
                 return scores + jnp.concatenate([bias] * 3, axis=1)
 
-            def last_old():
-                scores = score(queries, old_rows(jnp.minimum(whole, most_chunks - 1), 1))
-                key = lax.broadcasted_iota(jnp.int32, scores.shape, 0)
-                return jnp.where(key < ctx - whole * KEYS, scores, -1e30)
-
-            near[...] = new_scores(new_last)
-            top[...] = jnp.where(own_lane, jnp.max(near[...], axis=0, keepdims=True) * scale, 1e30)
-            mix(near[...], new_turned[new_last])
+            def higher(scores):
+                return jnp.max(scores, axis=0, keepdims=True)
+
+            scores = score(queries, old_rows(last, 1))
+            key = lax.broadcasted_iota(jnp.int32, scores.shape, 0)
+            near[pl.ds(KEYS, KEYS), :] = jnp.where(key < ctx - last * KEYS, scores, -1e30)
+            near[pl.ds(0, KEYS), :] = new_scores(new_last)
+            most = higher(near[...])
+            if exact:
+                most = lax.fori_loop(new_first, new_last, lambda i, m: jnp.maximum(m, higher(new_scores(i))), most)
+                most = lax.fori_loop(
+                    0, last, lambda i, m: jnp.maximum(m, higher(score(queries, old_rows(i, 1)))), most
+                )
+            top[...] = jnp.where(own_lane, most * scale, 1e30)
+            total[...] = jnp.zeros_like(total)
+            mixed[...] = jnp.zeros_like(mixed)
+            mix(near[...], jnp.concatenate([new_turned[new_last], old_turned[last]], axis=1))
 
             @pl.loop(new_first, new_last)
             def _(i):
                 mix(new_scores(i), new_turned[i])
 
+            def mix_old(i, count):
+                values = jnp.concatenate([old_turned[i + k] for k in range(count)], axis=1)
+                mix(score(queries, old_rows(i, count)), values)
+
             @pl.loop(0, long)
             def _(i):
-                values = jnp.concatenate([old_turned[i * LONG + k] for k in range(LONG)], axis=1)
-                mix(score(queries, old_rows(i * LONG, LONG)), values)
-
-            @pl.loop(long * LONG, whole)
-            def _(i):
-                mix(score(queries, old_rows(i, 1)), old_turned[i])
-
-            @pl.when(ctx > whole * KEYS)
+                mix_old(i * LONG, LONG)
+
+            @pl.when(last % LONG == 3)
             def _():
-                mix(last_old(), old_turned[whole])
-
-            @pl.when(jnp.max(jnp.where(own_lane, jnp.max(total[...], axis=0, keepdims=True), 0.0)) > 2.0**64)
+                mix_old(long * LONG, 3)
+
+            @pl.when(last % LONG == 2)
             def _():
-                def higher(scores):
-                    return jnp.max(scores, axis=0, keepdims=True)
-
-                most = higher(near[...])
-                most = lax.fori_loop(new_first, new_last, lambda i, m: jnp.maximum(m, higher(new_scores(i))), most)
-                most = lax.fori_loop(
-                    0, whole, lambda i, m: jnp.maximum(m, higher(score(queries, old_rows(i, 1)))), most
-                )
-                last = jnp.where(ctx > whole * KEYS, 0.0, -1e30)
-                most = jnp.maximum(most, higher(last_old()) + last)
-                top[...] = jnp.where(own_lane, most * scale, 1e30)
-                total[...] = jnp.zeros_like(total)
-                mixed[...] = jnp.zeros_like(mixed)
-
-                @pl.loop(new_first, new_last + 1)
-                def _(i):
-                    mix(new_scores(i), new_turned[i])
-
-                @pl.loop(0, whole)
-                def _(i):
-                    mix(score(queries, old_rows(i, 1)), old_turned[i])
-
-                @pl.when(ctx > whole * KEYS)
-                def _():
-                    mix(last_old(), old_turned[whole])
-
-            out = mixed[...] / jnp.sum(total[...], axis=0, keepdims=True)
+                mix_old(long * LONG, 2)
+
+            @pl.when(last % LONG == 1)
+            def _():
+                mix_old(long * LONG, 1)
+
+            weight = jnp.sum(total[...], axis=0, keepdims=True)
+            largest[...] = jnp.maximum(largest[...], jnp.where(own_lane, weight, 0.0))
+            out = mixed[...] / weight
             side = jnp.concatenate([out[:, h * TILE : (h + 1) * TILE] for h in range(3)], axis=0)
             row = lax.broadcasted_iota(jnp.int32, side.shape, 1) + first
             mine = (row >= begin) & (row < end)
@@ -306,6 +293,8 @@
             return 0
 
         lax.fori_loop(begin // TILE, (end + TILE - 1) // TILE, tile, 0)
+        if exact:
+            return end, packed
 
         def pack(i, _):
             dst = pl.ds(pl.multiple_of(packed + i * 16, 16), 16)
@@ -319,7 +308,12 @@
     kv_wide[pl.ds(tokens, 16), :] = jnp.zeros((16, 128), F32)
     kvx_ref[...] = jnp.zeros_like(kvx_ref)
     attn_turned[...] = jnp.zeros_like(attn_turned)
-    lax.fori_loop(0, 4, prompt, (0, 0))
+    largest[...] = jnp.zeros_like(largest)
+    lax.fori_loop(0, 4, functools.partial(prompt, exact=False), (0, 0))
+
+    @pl.when(jnp.logical_not(jnp.max(largest[...]) < 2.0**64))
+    def _():
+        lax.fori_loop(0, 4, functools.partial(prompt, exact=True), (0, 0))
 
     @pl.loop(0, tokens // TILE)
     def _(t):
@@ -357,13 +351,14 @@
         out_specs=(vmem(), vmem(), smem()),
         scratch_shapes=[
             pltpu.VMEM((tokens + 16, 128), F32),
-            pltpu.VMEM((cache.shape[1] // KEYS + 1, 64, KEYS), BF16),
+            pltpu.VMEM((cache.shape[1] // KEYS, 64, KEYS), BF16),
             pltpu.VMEM((tokens // KEYS, 64, KEYS), BF16),
             pltpu.VMEM((tokens // TILE, 192, TILE), F32),
-            pltpu.VMEM((KEYS, 3 * TILE), F32),
+            pltpu.VMEM((2 * KEYS, 3 * TILE), F32),
             pltpu.VMEM((1, 3 * TILE), F32),
             pltpu.VMEM((8, 3 * TILE), F32),
             pltpu.VMEM((64, 3 * TILE), F32),
+            pltpu.VMEM((1, 3 * TILE), F32),
         ],
         compiler_params=pltpu.CompilerParams(vmem_limit_bytes=VMEM_BYTES),
     )(q, kv, cache, routes_t, gates_t, span_t, ctx, req_prompt, cache_slot)
@@ -857,6 +852,39 @@
     )(attn, w_out, hidden, gain, kvx, place_rows, w_gate_up, w_down)
 
 
+def emit_kernel(rows_hbm, cache_hbm, rows_out, cache_out, rows_buf, cache_buf, rsem, wsem):
+    ways = [(rows_hbm, rows_buf, rows_out)]
+    for i in range(6):
+        some = pl.ds(3 * i, 3)
+        ways.append((cache_hbm.at[some], cache_buf.at[some], cache_out.at[some]))
+    reads = [pltpu.make_async_copy(a, b, rsem.at[i]) for i, (a, b, _) in enumerate(ways)]
+    writes = [pltpu.make_async_copy(b, c, wsem.at[i]) for i, (_, b, c) in enumerate(ways)]
+    for one in reads:
+        one.start()
+    for read, write in zip(reads, writes):
+        read.wait()
+        write.start()
+    for one in writes:
+        one.wait()
+
+
+def emit(rows, cache):
+    return pl.pallas_call(
+        emit_kernel,
+        name="emit",
+        out_shape=(jax.ShapeDtypeStruct(rows.shape, BF16), jax.ShapeDtypeStruct(cache.shape, BF16)),
+        in_specs=[anyspace()] * 2,
+        out_specs=(anyspace(), anyspace()),
+        scratch_shapes=[
+            pltpu.VMEM(rows.shape, BF16),
+            pltpu.VMEM(cache.shape, BF16),
+            pltpu.SemaphoreType.DMA((7,)),
+            pltpu.SemaphoreType.DMA((7,)),
+        ],
+        compiler_params=pltpu.CompilerParams(vmem_limit_bytes=16 * 1024 * 1024),
+    )(rows, cache)
+
+
 def body(
     hidden_in, attn_gain, w_query, keyvalue_weight, w_out, cache_kv, ctx_len, span_len,
     ffn_gain, routes, gate_weights, w_gate_up, w_down, req_prompt, cache_slot,
@@ -875,6 +903,7 @@
     layer_out, cache = finish(
         attn, w_out, hidden_in, ffn_gain, kvx, place_rows, w_gate_up, w_down
     )
+    layer_out, cache = emit(layer_out, cache)
     return (layer_out, cache.reshape(18, 512, 1, 128))
 
 

time: 232 us -> 186 us (0.80)
  Pallas kernels: 226 us -> 182 us
  local copies, waits for them, and re-layouts: 5.04 us -> 2.65 us
    pallas_call x1, Pallas kernels: 86.5 us -> 43.9 us  [attend(): pl.pallas_call(attend_kernel, name='attend', out_shape=(jax.ShapeDtypeStr...]
    pallas_call x1, Pallas kernels: 117 us -> 113 us  [finish(): pl.pallas_call(finish_kernel, name='finish', out_shape=(jax.ShapeDtypeStr...]
    pallas_call x0 -> x1, Pallas kernels: none -> 2.94 us  [emit(): pl.pallas_call(emit_kernel, name='emit', out_shape=(jax.ShapeDtypeStruct(...]
    unnamed x2 -> x4, local copies, waits for them, and re-layouts: 5.04 us -> 2.65 us
where the time goes in v5:
time: 186 us; the launch traced here: 185 us
  Pallas kernels  182 us (98%)
  local copies, waits for them, and re-layouts  2.65 us (1%)
    pallas_call x1, Pallas kernels, finish(): pl.pallas_call(finish_kernel, name='finish', out_shape=(jax.ShapeDtypeStr...  113 us
    pallas_call x1, Pallas kernels, attend(): pl.pallas_call(attend_kernel, name='attend', out_shape=(jax.ShapeDtypeStr...  43.9 us
    pallas_call x1, Pallas kernels, project_tokens(): pl.pallas_call(project_kernel, name='project_tokens', out_shape=(jax.Shap...  22.3 us

profile of v5, /device:TPU:0, one launch (start us, length us, event | category | flops | bytes accessed | tf_op | source)
XLA Modules:
  0.0 185.3 jit_solution(15122417593151787395)
XLA Ops:
  0.6 22.3 %project_tokens.1 = (bf16[1024,384]{1,0:T(8,128)(2,1)}, bf16[1024,128]{1,0:T(8,128)(2,1)}) custom-call(bf16[128,1536]{1,0:T(8,128)(2,1)} %hidden_ref.3, f32[1536]{0:T(1024)} %gain_ref.2, bf16[192,1536]{1,0:T(8,128)(2,1)} %bitcast.10, bf16[1536,128]{1,0:T(8,128)(2,1)} %bitcast.11, f32[1,128]{1,0:T(1,128)} %constant.2.clone.freq_ref, s32[4,16]{1,0:T(4,128)} %bitcast.12, ...), custom_call_target="tpu_custom_call" | custom-call | tf_op jit(solution)/shard_map/project_tokens/pallas_call | solution.py:160
  22.9 43.9 %attend.1 = (bf16[1024,192]{1,0:T(8,128)(2,1)}, bf16[1152,128]{1,0:T(8,128)(2,1)}, s32[2,18]{1,0:T(2,128)}) custom-call(bf16[1024,384]{1,0:T(8,128)(2,1)} %get-tuple-element.11.q_ref, bf16[1024,128]{1,0:T(8,128)(2,1)} %get-tuple-element.12.kv_ref, bf16[4,2048,128]{2,1,0:T(8,128)(2,1)} %bitcast.9, s32[8,128]{1,0:T(8,128)} %bitcast.14, ...), custom_call_target="tpu_custom_call" | custom-call | tf_op jit(solution)/shard_map/attend/pallas_call | solution.py:342
  66.8 112.7 %finish.1 = (bf16[128,1536]{1,0:T(8,128)(2,1)}, bf16[18,512,128]{2,1,0:T(8,128)(2,1)}) custom-call(bf16[1024,192]{1,0:T(8,128)(2,1)} %get-tuple-element.13.attn_ref, bf16[192,1536]{1,0:T(8,128)(2,1)} %wout_ref.1, bf16[128,1536]{1,0:T(8,128)(2,1)} %hidden_ref.3, f32[1536]{0:T(1024)} %gain_ref.3, bf16[1152,128]{1,0:T(8,128)(2,1)} %get-tuple-element.14.kvx_ref, ...), custom_call_target="tpu_custom_call" | custom-call | tf_op jit(solution)/shard_map/finish/pallas_call | solution.py:809
  179.5 0.0 copy-start
  179.5 1.7 copy-done
  181.2 0.0 copy-start.1
  181.2 1.0 copy-done.1
  182.2 2.9 %emit.1 = (bf16[128,1536]{1,0:T(8,128)(2,1)}, bf16[18,512,128]{2,1,0:T(8,128)(2,1)}) custom-call(bf16[128,1536]{1,0:T(8,128)(2,1)S(1)} %copy-done.1, bf16[18,512,128]{2,1,0:T(8,128)(2,1)S(1)} %copy-done), custom_call_target="tpu_custom_call" | custom-call | tf_op jit(solution)/shard_map/emit/pallas_call | solution.py:872
Async XLA Ops:
  179.5 1.7 copy-start
  181.2 1.0 copy-start.1
